TPU v7x, 256 devices: a whole 4x4x8 slice. The times are simulated.
256 devices in a mesh: geo: 32 (over x, z), bins: 8 (over y, core).
Axes of the slice: x: 4, y: 4, z: 8, core: 2. Of those that a mesh axis runs over, the one named last changes fastest.
Arguments:
- spectrum: float32 [1152, 256, 256], P('bins', 'geo'), may hold values from 0.1 to 2
- sea_mask: int32 [256, 256], P('geo'), may hold values 0 or 1
- kernel_linear: bfloat16 [1152, 1152], replicated, may hold values from -0.1875 to 0.1875
- kernel_square: bfloat16 [1152, 1152], replicated, may hold values from -0.1875 to 0.1875
- drift_kernel: bfloat16 [128, 1152], replicated, may hold values from -0.1875 to 0.1875
- ocean: float32 [2, 64, 256, 256], P(None, 'bins', 'geo'), may hold values from -3 to 3
Outputs:
- spectrum_out: float32 [1152, 256, 256], P('bins', 'geo')
- ocean_out: float32 [2, 64, 256, 256], P(None, 'bins', 'geo')
Inputs may be any that keep to these rules, and one draw needn't show every extreme that they name: `sea_mask`: 1 marks a sea column, 0 a land column.
All inputs are finite; a program needn't handle non-finite values. No bound on the sum of `sea_mask` on one device may be relied on, other than what follows from the above.
Results may differ from a plain program's by a relative error of at most 0.0018.
Values sent between devices are 32-bit elements; how exact they have to be, the bound alone decides.
A program may use at most 64 MiB of HBM per device.

v0:
```python
import jax
import jax.numpy as jnp
from jax import lax
from jax.sharding import PartitionSpec as P

NDIR = 36
NFREQ = 32
NB = 1152
STEPS = 3
SUB = 2


DT_SOURCE = 0.5
DT_OCEAN = 0.2
CORIOLIS = 1.0
VISCOSITY = 1.0
DOPPLER = 0.1


def broadcast(shard, axis, root):
    return lax.dynamic_index_in_dim(lax.all_gather(shard, axis), root, 0, keepdims=False)


def extended_2(shard, sides, width):
    for axis, dim in sides:
        size, length = (lax.axis_size(axis), shard.shape[dim])
        up = [(i, (i + 1) % size) for i in range(size)]
        down = [(j, i) for i, j in up]
        last = lax.slice_in_dim(shard, length - width, length, axis=dim)
        first = lax.slice_in_dim(shard, 0, width, axis=dim)
        before = lax.ppermute(last, axis, up)
        after = lax.ppermute(first, axis, down)
        shard = jnp.concatenate([before, shard, after], axis=dim)
    return shard


def speeds(first_bin, bin_count):
    bin_index = first_bin + jnp.arange(bin_count, dtype=jnp.int32)
    direction = (bin_index // NFREQ).astype(jnp.float32)
    frequency = (bin_index % NFREQ).astype(jnp.float32)
    group_speed = 0.4 / (1.0 + frequency / 16.0)
    bin_angle = 2.0 * jnp.pi / NDIR * direction
    return (group_speed * jnp.cos(bin_angle), group_speed * jnp.sin(bin_angle))


def along_y(energy, speed_y):
    flux_plus = jnp.maximum(speed_y, 0.0) * energy
    flux_minus = jnp.minimum(speed_y, 0.0) * energy
    zeros_edge = jnp.zeros_like(flux_plus[..., :1])
    plus_before = jnp.concatenate([zeros_edge, flux_plus[..., :-1]], axis=-1)
    minus_after = jnp.concatenate([flux_minus[..., 1:], zeros_edge], axis=-1)
    return flux_plus - plus_before + (minus_after - flux_minus)


def step_cells(energy, plus_left, flux_plus, flux_minus, minus_right, speed_y, sea_float):
    moved = energy - (flux_plus - plus_left + (minus_right - flux_minus)) - along_y(energy, speed_y)
    return moved * sea_float


def renew_source(energy, interaction, squares_sum, sea_float):
    return energy + DT_SOURCE * (sea_float * (interaction * energy / (1.0 + squares_sum / NB)))


def laplace(centre, west_side, east_side):
    zeros_edge = jnp.zeros_like(centre[..., :1])
    north_side = jnp.concatenate([centre[..., 1:], zeros_edge], axis=-1)
    south_side = jnp.concatenate([zeros_edge, centre[..., :-1]], axis=-1)
    return east_side + west_side + (north_side + south_side) - 4.0 * centre


def ocean_step(ocean_state, west_side, east_side, stokes_u, stokes_v, sea_float):
    laplacian = laplace(ocean_state, west_side, east_side)
    new_u = (
        ocean_state[0]
        + DT_OCEAN * (CORIOLIS * (ocean_state[1] + stokes_v) + VISCOSITY * laplacian[0])
    ) * sea_float
    new_v = (
        ocean_state[1]
        + DT_OCEAN * (-(CORIOLIS * (ocean_state[0] + stokes_u)) + VISCOSITY * laplacian[1])
    ) * sea_float
    return jnp.stack([new_u, new_v])


def per_device(spectrum, sea_mask, kernel_linear, kernel_square, drift_kernel, ocean):
    bin_count = spectrum.shape[0]
    width_x = spectrum.shape[1]
    width_y = spectrum.shape[2]
    columns = width_x * width_y
    levels = ocean.shape[1]
    bin_parts = lax.axis_size("bins")
    bin_rank = lax.axis_index("bins")
    first_bin = bin_rank * bin_count
    speed_cx, speed_cy = speeds(first_bin, bin_count)
    sea_float = sea_mask.astype(jnp.float32)
    energy = spectrum
    ocean_state = ocean
    for step_index in range(STEPS):
        current = broadcast(ocean_state[:, 0], "bins", 0)
        tanh_cur = jnp.tanh(current)
        stacked = jnp.concatenate([energy, tanh_cur, sea_float[None]], axis=0)
        widened = extended_2(stacked, (("geo", 1),), SUB)
        energy_wide = widened[:bin_count]
        tanh_east = widened[bin_count]
        tanh_north = widened[bin_count + 1]
        sea_wide = widened[bin_count + 2]
        for substep in range(SUB):
            speed_x = speed_cx[:, None, None] + DOPPLER * tanh_east[None]
            speed_y = speed_cy[:, None, None] + DOPPLER * tanh_north[None]
            flux_plus = jnp.maximum(speed_x, 0.0) * energy_wide
            flux_minus = jnp.minimum(speed_x, 0.0) * energy_wide
            energy_wide = step_cells(
                energy_wide[:, 1:-1],
                flux_plus[:, :-2],
                flux_plus[:, 1:-1],
                flux_minus[:, 1:-1],
                flux_minus[:, 2:],
                speed_y[:, 1:-1],
                sea_wide[1:-1],
            )
            tanh_east = tanh_east[1:-1]
            tanh_north = tanh_north[1:-1]
            sea_wide = sea_wide[1:-1]
        energy = energy_wide
        energy_flat = energy.reshape(bin_count, columns)
        gathered = lax.all_to_all(energy_flat, "bins", split_axis=1, concat_axis=0, tiled=True)
        col_share = columns // bin_parts
        sea_share = lax.dynamic_slice_in_dim(
            sea_float.reshape(columns), bin_rank * col_share, col_share
        )
        rounded = gathered.astype(jnp.bfloat16)
        squared = (gathered * gathered).astype(jnp.bfloat16)
        interaction = jnp.dot(kernel_linear, rounded, preferred_element_type=jnp.float32) + jnp.dot(
            kernel_square, squared, preferred_element_type=jnp.float32
        )
        updated = renew_source(
            gathered, interaction, jnp.sum(gathered * gathered, axis=0), sea_share
        )
        stokes_cols = jnp.dot(
            drift_kernel, updated.astype(jnp.bfloat16), preferred_element_type=jnp.float32
        )
        energy_flat, stokes_drift = (
            lax.all_to_all(updated, "bins", split_axis=0, concat_axis=1, tiled=True),
            lax.all_to_all(stokes_cols, "bins", split_axis=0, concat_axis=1, tiled=True),
        )
        energy = energy_flat.reshape(bin_count, width_x, width_y)
        stokes_drift = stokes_drift.reshape(levels, 2, width_x, width_y)
        extended = extended_2(ocean_state, (("geo", 2),), 1)
        ocean_state = ocean_step(
            ocean_state,
            extended[:, :, :-2],
            extended[:, :, 2:],
            stokes_drift[:, 0],
            stokes_drift[:, 1],
            sea_float,
        )
    return (energy, ocean_state)


def solution(mesh):
    return jax.shard_map(
        per_device,
        mesh=mesh,
        in_specs=(
            P("bins", "geo", None),
            P("geo", None),
            P(),
            P(),
            P(),
            P(None, "bins", "geo", None),
        ),
        out_specs=(P("bins", "geo", None), P(None, "bins", "geo", None)),
        check_vma=False,
    )
```

profile of v0, /device:TPU:1, one launch (start us, length us, event | category | flops | bytes accessed | tf_op | source)
XLA Modules:
  0.0 296.8 jit_solution(13492282019533903558)
XLA Ops:
  1.5 1.7 copy.46
  3.2 15.8 %all-gather = f32[16,1,8,256]{3,2,1,0:T(8,128)S(1)} all-gather(f32[2,1,8,256]{3,2,1,0:T(8,128)S(1)} %slice-done), channel_id=2, replica_groups=mesh['geo'=32,'bins'=8] {'bins'}, dimensions={0}, use_global_device_ids=true | all-gather | bytes 147456 | tf_op jit(solution)/shard_map/all_gather | solution.py:21
  20.5 6.1 %collective-permute-start.1 = (f32[147,2,256]{2,0,1:T(8,128)}, f32[147,2,256]{2,0,1:T(8,128)}, u32[]{:S(2)}, u32[]{:S(2)}) collective-permute-start(f32[147,2,256]{2,0,1:T(8,128)} %get-tuple-element.50), channel_id=1, source_target_pairs={{8,0},{16,8},{24,16},{32,24},{40,32},{48,40},{56,48},{64,56},{72,6... | collective-permute-start | bytes 903176 | tf_op jit(solution)/shard_map/ppermute | solution.py:32
  26.7 7.7 %collective-permute-done = f32[147,2,256]{2,0,1:T(8,128)S(1)} collective-permute-done((f32[147,2,256]{2,0,1:T(8,128)}, f32[147,2,256]{2,0,1:T(8,128)S(1)}, u32[]{:S(2)}, u32[]{:S(2)}) %collective-permute-start) | collective-permute-done | bytes 301088 | tf_op jit(solution)/shard_map/ppermute | solution.py:31
  34.4 1.5 fusion.19
  39.6 1.9 fusion.71
  41.5 4.9 %all-to-all-start = ((f32[144,8,256]{2,0,1:T(8,128)}), f32[144,8,256]{2,0,1:T(8,128)}, u32[]{:S(2)}, u32[]{:S(2)}) async-start(f32[144,8,256]{2,0,1:T(8,128)} %fusion.71), calls=%async_computation | async-start | bytes 2359296 | tf_op jit(solution)/shard_map/all_to_all | solution.py:125
  46.5 16.4 %all-to-all-done = f32[144,8,256]{2,0,1:T(8,128)} async-done(((f32[144,8,256]{2,0,1:T(8,128)}), f32[144,8,256]{2,0,1:T(8,128)}, u32[]{:S(2)}, u32[]{:S(2)}) %all-to-all-start) | async-done | bytes 1179680 | tf_op jit(solution)/shard_map/all_to_all | solution.py:125
  62.9 2.7 copy.48
  65.6 2.5 fusion.85
  68.1 1.4 fusion.74
  69.5 2.6 fusion.17
  74.1 4.2 %all-to-all-start.2 = ((f32[8,16,256]{2,1,0:T(8,128)}), f32[8,16,256]{2,1,0:T(8,128)S(1)}, u32[]{:S(2)}, u32[]{:S(2)}) async-start(f32[8,16,256]{2,1,0:T(8,128)} %bitcast.8), calls=%async_computation.2 | async-start | bytes 262144 | tf_op jit(solution)/shard_map/all_to_all | solution.py:143
  78.4 5.0 %collective-permute-start.2 = (f32[2,8,1,256]{3,2,1,0:T(1,128)S(1)}, f32[2,8,1,256]{3,2,1,0:T(1,128)S(1)}, u32[]{:S(2)}, u32[]{:S(2)}) collective-permute-start(f32[2,8,1,256]{3,2,1,0:T(1,128)S(1)} %get-tuple-element.67), channel_id=1, source_target_pairs={{8,0},{16,8},{24,16},{32,24},{40,32},{48,40},{56,48},{64,56},{72,6... | collective-permute-start | bytes 49160 | tf_op jit(solution)/shard_map/ppermute | solution.py:32
  83.6 2.7 copy.49
  86.3 5.1 %all-to-all-start.1 = ((f32[8,144,256]{2,1,0:T(8,128)}), f32[8,144,256]{2,1,0:T(8,128)}, u32[]{:S(2)}, u32[]{:S(2)}) async-start(f32[8,144,256]{2,1,0:T(8,128)} %bitcast.212), calls=%async_computation.1 | async-start | bytes 2359296 | tf_op jit(solution)/shard_map/all_to_all | solution.py:142
  91.7 22.7 %all-gather.1 = f32[16,1,8,256]{3,2,1,0:T(8,128)S(1)} all-gather(f32[2,1,8,256]{3,2,1,0:T(8,128)S(1)} %fusion.132), channel_id=3, replica_groups=mesh['geo'=32,'bins'=8] {'bins'}, dimensions={0}, use_global_device_ids=true | all-gather | bytes 147456 | tf_op jit(solution)/shard_map/all_gather | solution.py:21
  114.5 1.4 pad_maximum_fusion.4
  116.0 5.1 %collective-permute-start.5 = (f32[147,2,256]{2,0,1:T(8,128)S(1)}, f32[147,2,256]{2,0,1:T(8,128)S(1)}, u32[]{:S(2)}, u32[]{:S(2)}) collective-permute-start(f32[147,2,256]{2,0,1:T(8,128)S(1)} %get-tuple-element.48), channel_id=1, source_target_pairs={{8,0},{16,8},{24,16},{32,24},{40,32},{48,40},{56,48},{64,56},{72,6... | collective-permute-start | bytes 903176 | tf_op jit(solution)/shard_map/ppermute | solution.py:32
  121.1 7.5 %collective-permute-done.4 = f32[147,2,256]{2,0,1:T(8,128)S(1)} collective-permute-done((f32[147,2,256]{2,0,1:T(8,128)S(1)}, f32[147,2,256]{2,0,1:T(8,128)S(1)}, u32[]{:S(2)}, u32[]{:S(2)}) %collective-permute-start.4) | collective-permute-done | bytes 301088 | tf_op jit(solution)/shard_map/ppermute | solution.py:31
  128.6 1.4 fusion.21
  134.6 20.5 %all_to_all.144 = f32[144,8,256]{2,0,1:T(8,128)} all-to-all(f32[144,8,256]{2,0,1:T(8,128)S(1)} %fusion.67), channel_id=1, replica_groups=mesh['geo'=32,'bins'=8] {'bins'}, dimensions={1} | all-to-all | bytes 2359296 | tf_op jit(solution)/shard_map/all_to_all | solution.py:125
  155.2 2.7 copy.54
  157.8 2.5 fusion.81
  160.6 1.2 fusion.13
  163.9 4.1 %all-to-all-start.5 = ((f32[8,16,256]{2,1,0:T(8,128)}), f32[8,16,256]{2,1,0:T(8,128)S(1)}, u32[]{:S(2)}, u32[]{:S(2)}) async-start(f32[8,16,256]{2,1,0:T(8,128)} %bitcast.22), calls=%async_computation.5 | async-start | bytes 262144 | tf_op jit(solution)/shard_map/all_to_all | solution.py:143
  168.0 2.7 copy.55
  170.7 2.6 all-to-all-done.5
  173.3 5.0 %all-to-all-start.4 = ((f32[8,144,256]{2,1,0:T(8,128)}), f32[8,144,256]{2,1,0:T(8,128)}, u32[]{:S(2)}, u32[]{:S(2)}) async-start(f32[8,144,256]{2,1,0:T(8,128)} %bitcast.210), calls=%async_computation.4 | async-start | bytes 2359296 | tf_op jit(solution)/shard_map/all_to_all | solution.py:142
  178.3 5.0 %collective-permute-start.6 = (f32[2,8,1,256]{3,2,1,0:T(1,128)S(1)}, f32[2,8,1,256]{3,2,1,0:T(1,128)S(1)}, u32[]{:S(2)}, u32[]{:S(2)}) collective-permute-start(f32[2,8,1,256]{3,2,1,0:T(1,128)S(1)} %get-tuple-element.63), channel_id=1, source_target_pairs={{8,0},{16,8},{24,16},{32,24},{40,32},{48,40},{56,48},{64,56},{72,6... | collective-permute-start | bytes 49160 | tf_op jit(solution)/shard_map/ppermute | solution.py:32
  183.3 9.0 %collective-permute-start.7 = (f32[2,8,1,256]{3,2,1,0:T(1,128)S(1)}, f32[2,8,1,256]{3,2,1,0:T(1,128)S(1)}, u32[]{:S(2)}, u32[]{:S(2)}) collective-permute-start(f32[2,8,1,256]{3,2,1,0:T(1,128)S(1)} %get-tuple-element.64), channel_id=1, source_target_pairs={{0,8},{8,16},{16,24},{24,32},{32,40},{40,48},{48,56},{56,64},{64,7... | collective-permute-start | bytes 49160 | tf_op jit(solution)/shard_map/ppermute | solution.py:31
  192.3 5.8 %collective-permute-done.7 = f32[2,8,1,256]{3,2,1,0:T(1,128)S(1)} collective-permute-done((f32[2,8,1,256]{3,2,1,0:T(1,128)S(1)}, f32[2,8,1,256]{3,2,1,0:T(1,128)S(1)}, u32[]{:S(2)}, u32[]{:S(2)}) %collective-permute-start.7) | collective-permute-done | bytes 16416 | tf_op jit(solution)/shard_map/ppermute | solution.py:31
  198.4 14.9 %all-gather.2 = f32[16,1,8,256]{3,2,1,0:T(8,128)S(1)} all-gather(f32[2,1,8,256]{3,2,1,0:T(8,128)S(1)} %fusion.129), channel_id=4, replica_groups=mesh['geo'=32,'bins'=8] {'bins'}, dimensions={0}, use_global_device_ids=true | all-gather | bytes 147456 | tf_op jit(solution)/shard_map/all_gather | solution.py:21
  213.3 1.4 pad_maximum_fusion.3
  214.8 4.8 %collective-permute-start.9 = (f32[147,2,256]{2,0,1:T(8,128)S(1)}, f32[147,2,256]{2,0,1:T(8,128)S(1)}, u32[]{:S(2)}, u32[]{:S(2)}) collective-permute-start(f32[147,2,256]{2,0,1:T(8,128)S(1)} %get-tuple-element.46), channel_id=1, source_target_pairs={{8,0},{16,8},{24,16},{32,24},{40,32},{48,40},{56,48},{64,56},{72,6... | collective-permute-start | bytes 903176 | tf_op jit(solution)/shard_map/ppermute | solution.py:32
  219.6 7.3 %collective-permute-done.8 = f32[147,2,256]{2,0,1:T(8,128)S(1)} collective-permute-done((f32[147,2,256]{2,0,1:T(8,128)S(1)}, f32[147,2,256]{2,0,1:T(8,128)S(1)}, u32[]{:S(2)}, u32[]{:S(2)}) %collective-permute-start.8) | collective-permute-done | bytes 301088 | tf_op jit(solution)/shard_map/ppermute | solution.py:31
  226.9 1.4 fusion.23
  232.9 21.1 %all_to_all.145 = f32[144,8,256]{2,0,1:T(8,128)} all-to-all(f32[144,8,256]{2,0,1:T(8,128)S(1)} %fusion.63), channel_id=1, replica_groups=mesh['geo'=32,'bins'=8] {'bins'}, dimensions={1} | all-to-all | bytes 2359296 | tf_op jit(solution)/shard_map/all_to_all | solution.py:125
  254.0 2.7 copy.61
  256.7 2.5 fusion.77
  262.8 4.1 %all-to-all-start.8 = ((f32[8,16,256]{2,1,0:T(8,128)}), f32[8,16,256]{2,1,0:T(8,128)S(1)}, u32[]{:S(2)}, u32[]{:S(2)}) async-start(f32[8,16,256]{2,1,0:T(8,128)} %bitcast.36), calls=%async_computation.8 | async-start | bytes 262144 | tf_op jit(solution)/shard_map/all_to_all | solution.py:143
  266.9 2.7 copy.62
  269.6 2.6 all-to-all-done.8
  272.2 5.0 %all-to-all-start.7 = ((f32[8,144,256]{2,1,0:T(8,128)}), f32[8,144,256]{2,1,0:T(8,128)}, u32[]{:S(2)}, u32[]{:S(2)}) async-start(f32[8,144,256]{2,1,0:T(8,128)} %bitcast.211), calls=%async_computation.7 | async-start | bytes 2359296 | tf_op jit(solution)/shard_map/all_to_all | solution.py:142
  277.2 4.9 %collective-permute-start.10 = (f32[2,8,1,256]{3,2,1,0:T(1,128)S(1)}, f32[2,8,1,256]{3,2,1,0:T(1,128)S(1)}, u32[]{:S(2)}, u32[]{:S(2)}) collective-permute-start(f32[2,8,1,256]{3,2,1,0:T(1,128)S(1)} %get-tuple-element.59), channel_id=1, source_target_pairs={{8,0},{16,8},{24,16},{32,24},{40,32},{48,40},{56,48},{64,56},{72,6... | collective-permute-start | bytes 49160 | tf_op jit(solution)/shard_map/ppermute | solution.py:32
  282.9 5.0 %collective-permute-done.11 = f32[2,8,1,256]{3,2,1,0:T(1,128)S(1)} collective-permute-done((f32[2,8,1,256]{3,2,1,0:T(1,128)S(1)}, f32[2,8,1,256]{3,2,1,0:T(1,128)S(1)}, u32[]{:S(2)}, u32[]{:S(2)}) %collective-permute-start.11) | collective-permute-done | bytes 16416 | tf_op jit(solution)/shard_map/ppermute | solution.py:31
  288.9 4.8 %all-to-all-done.7 = f32[8,144,256]{2,1,0:T(8,128)} async-done(((f32[8,144,256]{2,1,0:T(8,128)}), f32[8,144,256]{2,1,0:T(8,128)}, u32[]{:S(2)}, u32[]{:S(2)}) %all-to-all-start.7) | async-done | bytes 1179680 | tf_op jit(solution)/shard_map/all_to_all | solution.py:142
  293.7 3.0 %copy.66 = f32[144,8,256]{2,1,0:T(8,128)} copy(f32[144,8,256]{2,0,1:T(8,128)} %bitcast.34) | data formatting | bytes 2359296
  (137 shorter events, 26.1 us)
Async XLA Ops:
  0.6 64.9 %copy-start = (bf16[1152,1152]{1,0:T(8,128)(2,1)S(1)}, bf16[1152,1152]{1,0:T(8,128)(2,1)}, u32[]{:S(2)}) copy-start(bf16[1152,1152]{1,0:T(8,128)(2,1)} %param.8) | copy-start | bytes 7962628
  0.6 2.5 slice-start
  3.2 16.9 %copy-start.3 = (f32[144,8,256]{2,0,1:T(8,128)}, f32[144,8,256]{2,0,1:T(8,128)S(1)}, u32[]{:S(2)}) copy-start(f32[144,8,256]{2,0,1:T(8,128)S(1)} %copy.46) | copy-start | bytes 3538948
  20.0 14.4 %collective-permute-start = (f32[147,2,256]{2,0,1:T(8,128)}, f32[147,2,256]{2,0,1:T(8,128)S(1)}, u32[]{:S(2)}, u32[]{:S(2)}) collective-permute-start(f32[147,2,256]{2,0,1:T(8,128)} %get-tuple-element.49), channel_id=1, source_target_pairs={{0,8},{8,16},{16,24},{24,32},{32,40},{40,48},{48,56},{56,64},{64,7... | collective-permute-start | bytes 903176 | tf_op jit(solution)/shard_map/ppermute | solution.py:31
  20.5 13.9 %collective-permute-start.1 = (f32[147,2,256]{2,0,1:T(8,128)}, f32[147,2,256]{2,0,1:T(8,128)}, u32[]{:S(2)}, u32[]{:S(2)}) collective-permute-start(f32[147,2,256]{2,0,1:T(8,128)} %get-tuple-element.50), channel_id=1, source_target_pairs={{8,0},{16,8},{24,16},{32,24},{40,32},{48,40},{56,48},{64,56},{72,6... | collective-permute-start | bytes 903176 | tf_op jit(solution)/shard_map/ppermute | solution.py:32
  41.5 21.4 %all-to-all-start = ((f32[144,8,256]{2,0,1:T(8,128)}), f32[144,8,256]{2,0,1:T(8,128)}, u32[]{:S(2)}, u32[]{:S(2)}) async-start(f32[144,8,256]{2,0,1:T(8,128)} %fusion.71), calls=%async_computation | async-start | bytes 2359296 | tf_op jit(solution)/shard_map/all_to_all | solution.py:125
  65.6 3.9 %copy-start.10 = (f32[1152,256]{0,1:T(8,128)S(1)}, f32[1152,256]{0,1:T(8,128)}, u32[]{:S(2)}) copy-start(f32[1152,256]{0,1:T(8,128)} %copy.48) | copy-start | bytes 3538948
  65.6 3.9 %copy-start.12 = (bf16[1152,1152]{1,0:T(8,128)(2,1)S(1)}, bf16[1152,1152]{1,0:T(8,128)(2,1)}, u32[]{:S(2)}) copy-start(bf16[1152,1152]{1,0:T(8,128)(2,1)} %param.9) | copy-start | bytes 7962628
  69.5 3.6 %copy-start.7 = (bf16[128,1152]{1,0:T(8,128)(2,1)S(1)}, bf16[128,1152]{1,0:T(8,128)(2,1)}, u32[]{:S(2)}) copy-start(bf16[128,1152]{1,0:T(8,128)(2,1)} %param.10) | copy-start | bytes 884740
  72.1 1.0 copy-start.4
  73.1 5.2 %copy-start.8 = (f32[2,8,8,256]{3,2,1,0:T(8,128)S(1)}, f32[2,8,8,256]{3,2,1,0:T(8,128)}, u32[]{:S(2)}) copy-start(f32[2,8,8,256]{3,2,1,0:T(8,128)} %param.11) | copy-start | bytes 393220
  74.1 12.1 %all-to-all-start.2 = ((f32[8,16,256]{2,1,0:T(8,128)}), f32[8,16,256]{2,1,0:T(8,128)S(1)}, u32[]{:S(2)}, u32[]{:S(2)}) async-start(f32[8,16,256]{2,1,0:T(8,128)} %bitcast.8), calls=%async_computation.2 | async-start | bytes 262144 | tf_op jit(solution)/shard_map/all_to_all | solution.py:143
  78.4 13.1 %collective-permute-start.2 = (f32[2,8,1,256]{3,2,1,0:T(1,128)S(1)}, f32[2,8,1,256]{3,2,1,0:T(1,128)S(1)}, u32[]{:S(2)}, u32[]{:S(2)}) collective-permute-start(f32[2,8,1,256]{3,2,1,0:T(1,128)S(1)} %get-tuple-element.67), channel_id=1, source_target_pairs={{8,0},{16,8},{24,16},{32,24},{40,32},{48,40},{56,48},{64,56},{72,6... | collective-permute-start | bytes 49160 | tf_op jit(solution)/shard_map/ppermute | solution.py:32
  83.4 8.1 %collective-permute-start.3 = (f32[2,8,1,256]{3,2,1,0:T(1,128)S(1)}, f32[2,8,1,256]{3,2,1,0:T(1,128)S(1)}, u32[]{:S(2)}, u32[]{:S(2)}) collective-permute-start(f32[2,8,1,256]{3,2,1,0:T(1,128)S(1)} %get-tuple-element.68), channel_id=1, source_target_pairs={{0,8},{8,16},{16,24},{24,32},{32,40},{40,48},{48,56},{56,64},{64,7... | collective-permute-start | bytes 49160 | tf_op jit(solution)/shard_map/ppermute | solution.py:31
  86.3 28.2 %all-to-all-start.1 = ((f32[8,144,256]{2,1,0:T(8,128)}), f32[8,144,256]{2,1,0:T(8,128)}, u32[]{:S(2)}, u32[]{:S(2)}) async-start(f32[8,144,256]{2,1,0:T(8,128)} %bitcast.212), calls=%async_computation.1 | async-start | bytes 2359296 | tf_op jit(solution)/shard_map/all_to_all | solution.py:142
  115.9 12.7 %collective-permute-start.4 = (f32[147,2,256]{2,0,1:T(8,128)S(1)}, f32[147,2,256]{2,0,1:T(8,128)S(1)}, u32[]{:S(2)}, u32[]{:S(2)}) collective-permute-start(f32[147,2,256]{2,0,1:T(8,128)S(1)} %get-tuple-element.47), channel_id=1, source_target_pairs={{0,8},{8,16},{16,24},{24,32},{32,40},{40,48},{48,56},{56,64},{64,7... | collective-permute-start | bytes 903176 | tf_op jit(solution)/shard_map/ppermute | solution.py:31
  116.0 12.6 %collective-permute-start.5 = (f32[147,2,256]{2,0,1:T(8,128)S(1)}, f32[147,2,256]{2,0,1:T(8,128)S(1)}, u32[]{:S(2)}, u32[]{:S(2)}) collective-permute-start(f32[147,2,256]{2,0,1:T(8,128)S(1)} %get-tuple-element.48), channel_id=1, source_target_pairs={{8,0},{16,8},{24,16},{32,24},{40,32},{48,40},{56,48},{64,56},{72,6... | collective-permute-start | bytes 903176 | tf_op jit(solution)/shard_map/ppermute | solution.py:32
  157.8 2.5 copy-start.2
  157.8 2.7 copy-start.11
  157.8 2.8 copy-start.13
  161.9 1.0 copy-start.6
  163.9 9.4 %all-to-all-start.5 = ((f32[8,16,256]{2,1,0:T(8,128)}), f32[8,16,256]{2,1,0:T(8,128)S(1)}, u32[]{:S(2)}, u32[]{:S(2)}) async-start(f32[8,16,256]{2,1,0:T(8,128)} %bitcast.22), calls=%async_computation.5 | async-start | bytes 262144 | tf_op jit(solution)/shard_map/all_to_all | solution.py:143
  173.3 40.0 %all-to-all-start.4 = ((f32[8,144,256]{2,1,0:T(8,128)}), f32[8,144,256]{2,1,0:T(8,128)}, u32[]{:S(2)}, u32[]{:S(2)}) async-start(f32[8,144,256]{2,1,0:T(8,128)} %bitcast.210), calls=%async_computation.4 | async-start | bytes 2359296 | tf_op jit(solution)/shard_map/all_to_all | solution.py:142
  178.3 14.0 %collective-permute-start.6 = (f32[2,8,1,256]{3,2,1,0:T(1,128)S(1)}, f32[2,8,1,256]{3,2,1,0:T(1,128)S(1)}, u32[]{:S(2)}, u32[]{:S(2)}) collective-permute-start(f32[2,8,1,256]{3,2,1,0:T(1,128)S(1)} %get-tuple-element.63), channel_id=1, source_target_pairs={{8,0},{16,8},{24,16},{32,24},{40,32},{48,40},{56,48},{64,56},{72,6... | collective-permute-start | bytes 49160 | tf_op jit(solution)/shard_map/ppermute | solution.py:32
  183.3 14.9 %collective-permute-start.7 = (f32[2,8,1,256]{3,2,1,0:T(1,128)S(1)}, f32[2,8,1,256]{3,2,1,0:T(1,128)S(1)}, u32[]{:S(2)}, u32[]{:S(2)}) collective-permute-start(f32[2,8,1,256]{3,2,1,0:T(1,128)S(1)} %get-tuple-element.64), channel_id=1, source_target_pairs={{0,8},{8,16},{16,24},{24,32},{32,40},{40,48},{48,56},{56,64},{64,7... | collective-permute-start | bytes 49160 | tf_op jit(solution)/shard_map/ppermute | solution.py:31
  214.7 12.1 %collective-permute-start.8 = (f32[147,2,256]{2,0,1:T(8,128)S(1)}, f32[147,2,256]{2,0,1:T(8,128)S(1)}, u32[]{:S(2)}, u32[]{:S(2)}) collective-permute-start(f32[147,2,256]{2,0,1:T(8,128)S(1)} %get-tuple-element.45), channel_id=1, source_target_pairs={{0,8},{8,16},{16,24},{24,32},{32,40},{40,48},{48,56},{56,64},{64,7... | collective-permute-start | bytes 903176 | tf_op jit(solution)/shard_map/ppermute | solution.py:31
  214.8 12.1 %collective-permute-start.9 = (f32[147,2,256]{2,0,1:T(8,128)S(1)}, f32[147,2,256]{2,0,1:T(8,128)S(1)}, u32[]{:S(2)}, u32[]{:S(2)}) collective-permute-start(f32[147,2,256]{2,0,1:T(8,128)S(1)} %get-tuple-element.46), channel_id=1, source_target_pairs={{8,0},{16,8},{24,16},{32,24},{40,32},{48,40},{56,48},{64,56},{72,6... | collective-permute-start | bytes 903176 | tf_op jit(solution)/shard_map/ppermute | solution.py:32
  256.7 2.5 copy-start.1
  256.7 2.7 copy-start.9
  256.7 2.8 copy-start.14
  260.8 1.0 copy-start.5
  262.8 9.4 %all-to-all-start.8 = ((f32[8,16,256]{2,1,0:T(8,128)}), f32[8,16,256]{2,1,0:T(8,128)S(1)}, u32[]{:S(2)}, u32[]{:S(2)}) async-start(f32[8,16,256]{2,1,0:T(8,128)} %bitcast.36), calls=%async_computation.8 | async-start | bytes 262144 | tf_op jit(solution)/shard_map/all_to_all | solution.py:143
  272.2 21.5 %all-to-all-start.7 = ((f32[8,144,256]{2,1,0:T(8,128)}), f32[8,144,256]{2,1,0:T(8,128)}, u32[]{:S(2)}, u32[]{:S(2)}) async-start(f32[8,144,256]{2,1,0:T(8,128)} %bitcast.211), calls=%async_computation.7 | async-start | bytes 2359296 | tf_op jit(solution)/shard_map/all_to_all | solution.py:142
  277.2 5.7 %collective-permute-start.10 = (f32[2,8,1,256]{3,2,1,0:T(1,128)S(1)}, f32[2,8,1,256]{3,2,1,0:T(1,128)S(1)}, u32[]{:S(2)}, u32[]{:S(2)}) collective-permute-start(f32[2,8,1,256]{3,2,1,0:T(1,128)S(1)} %get-tuple-element.59), channel_id=1, source_target_pairs={{8,0},{16,8},{24,16},{32,24},{40,32},{48,40},{56,48},{64,56},{72,6... | collective-permute-start | bytes 49160 | tf_op jit(solution)/shard_map/ppermute | solution.py:32
  282.0 5.9 %collective-permute-start.11 = (f32[2,8,1,256]{3,2,1,0:T(1,128)S(1)}, f32[2,8,1,256]{3,2,1,0:T(1,128)S(1)}, u32[]{:S(2)}, u32[]{:S(2)}) collective-permute-start(f32[2,8,1,256]{3,2,1,0:T(1,128)S(1)} %get-tuple-element.60), channel_id=1, source_target_pairs={{0,8},{8,16},{16,24},{24,32},{32,40},{40,48},{48,56},{56,64},{64,7... | collective-permute-start | bytes 49160 | tf_op jit(solution)/shard_map/ppermute | solution.py:31
where the time goes:
time: 302 us; the launch traced here: 297 us
  blocking collectives  95 us (31%)
  starting transfers between devices  73.1 us (24%)
  waiting for transfers between devices  60.5 us (20%)
  local copies, waits for them, and re-layouts  28 us (9%)
  other arithmetic  23.3 us (8%)
  matrix products  15.4 us (5%)
    all_gather x3, blocking collectives, broadcast(): lax.all_gather(shard, axis)  53.4 us
    all_to_all x2, blocking collectives, per_device(): lax.all_to_all(energy_flat, 'bins', split_axis=1, concat_axis=0, tiled=True)  41.6 us
    ppermute x6, waiting for transfers between devices, extended_2(): before = lax.ppermute(last, axis, up)  33.3 us
    ppermute x6, starting transfers between devices, extended_2(): after = lax.ppermute(first, axis, down)  30.8 us
    all_to_all x1, waiting for transfers between devices, per_device(): lax.all_to_all(energy_flat, 'bins', split_axis=1, concat_axis=0, tiled=True)  16.4 us
    all_to_all x3, starting transfers between devices, per_device(): lax.all_to_all(updated, 'bins', split_axis=0, concat_axis=1, tiled=True)  15.1 us
    all_to_all x3, starting transfers between devices, per_device(): lax.all_to_all(stokes_cols, 'bins', split_axis=0, concat_axis=1, tiled=True)  12.5 us
    ppermute x6, starting transfers between devices, extended_2(): before = lax.ppermute(last, axis, up)  9.83 us
  transfers between devices with their start and end apart: 19, of which 10 were waited for; matrix products, arithmetic and copies ran while one was open for 3% of the time, Pallas kernels for 0%

commit v1 on v0

v1 whole, which is shorter than its diff:
```python
import jax
import jax.numpy as jnp
import numpy as np
from jax import lax
from jax.experimental import pallas as pl
from jax.experimental.pallas import tpu as pltpu
from jax.sharding import PartitionSpec as P

NDIR = 36
NFREQ = 32
NB = 1152
STEPS = 3
PARTS = 8
BINS = NB // PARTS
CHAN = 16
WX = 8
WY = 32
COLS = WX * WY
LT = NB // 128
OT = LT
NT = LT + 1
ROW = 40
ROWS = 13
EXT = ROW * ROWS
FIRST = 3

DT_SOURCE = 0.5
DT_OCEAN = 0.2
DOPPLER = 0.1

MESH = pl.DeviceIdType.MESH
TRANSPOSED = (((1,), (1,)), ((), ()))


def group_speeds():
    index = np.arange(NB)
    direction = (index // NFREQ).astype(np.float32)
    frequency = (index % NFREQ).astype(np.float32)
    speed = np.float32(0.4) / (np.float32(1.0) + frequency / np.float32(16.0))
    angle = np.float32(2.0 * np.pi / NDIR) * direction
    both = np.stack([speed * np.cos(angle), speed * np.sin(angle)]).astype(np.float32)
    return np.ascontiguousarray(np.broadcast_to(both.reshape(2, LT, 1, 128), (2, LT, 8, 128)))


def own_row(x):
    return pl.multiple_of((FIRST + x) * ROW, 8)


def kernel(
    xs, os, sea, kl, ks, dk, cg, eo, oo,
    flat, ext, sea_ext, e1, e2, rounded, squared, tu, tv, weight, drift,
    klv, ksv, dkv, ysend, yrecv, csend, crecv, sysend, syrecv, scsend, screcv,
    in_send, in_recv, halo_send, halo_recv, sea_send, sea_recv, out_send, out_recv, local,
):
    g = lax.axis_index("geo")
    r = lax.axis_index("bins")
    tiles = lax.axis_size("geo")
    west, east = lax.rem(g + tiles - 1, tiles), lax.rem(g + 1, tiles)
    south, north = lax.rem(r + PARTS - 1, PARTS), lax.rem(r + 1, PARTS)

    weights = [
        pltpu.make_async_copy(kl, klv, local.at[0]),
        pltpu.make_async_copy(ks, ksv, local.at[1]),
        pltpu.make_async_copy(dk, dkv, local.at[2]),
    ]
    own_in = [
        pltpu.make_async_copy(xs.at[r], flat.at[pl.ds(pl.multiple_of(r * BINS, 8), BINS)], local.at[3]),
        pltpu.make_async_copy(os.at[r], flat.at[pl.ds(pl.multiple_of(NB + r * CHAN, 8), CHAN)], local.at[4]),
    ]
    for copy in own_in + weights:
        copy.start()

    barrier = pltpu.get_barrier_semaphore()
    friends = [(g, lax.rem(r + d, PARTS)) for d in range(1, PARTS)]
    friends += [(x, y) for x in (west, east) for y in (south, r, north)]
    for friend in friends:
        pl.semaphore_signal(barrier, inc=1, device_id=friend, device_id_type=MESH)
    pl.semaphore_wait(barrier, len(friends))

    def remote(src, dst, send, recv, device):
        return pltpu.make_async_remote_copy(
            src_ref=src, dst_ref=dst, send_sem=send, recv_sem=recv, device_id=device, device_id_type=MESH
        )

    entering = []
    for d in range(1, PARTS):
        peer = lax.rem(r + d, PARTS)
        entering.append(remote(
            os.at[peer], flat.at[pl.ds(pl.multiple_of(NB + r * CHAN, 8), CHAN)],
            in_send.at[0, d], in_recv.at[0, d], (g, peer)))
        entering.append(remote(
            xs.at[peer], flat.at[pl.ds(pl.multiple_of(r * BINS, 8), BINS)],
            in_send.at[1, d], in_recv.at[1, d], (g, peer)))
    for copy in entering:
        copy.start()

    def halo_copies(field, ys, yr, cs, cr, send, recv):
        depth = field.shape[0]
        every = pl.ds(0, depth)
        copies = []
        for i in range(2):
            copies.append(remote(
                field.at[every, pl.ds((FIRST + i) * ROW, WY)],
                field.at[every, pl.ds((FIRST + WX + i) * ROW, WY)],
                send.at[i], recv.at[i], (west, r)))
            copies.append(remote(
                field.at[every, pl.ds((FIRST + WX - 2 + i) * ROW, WY)],
                field.at[every, pl.ds((FIRST - 2 + i) * ROW, WY)],
                send.at[2 + i], recv.at[2 + i], (east, r)))
        copies.append(remote(ys.at[0], yr.at[1], send.at[4], recv.at[4], (g, south)))
        copies.append(remote(ys.at[1], yr.at[0], send.at[5], recv.at[5], (g, north)))
        copies.append(remote(cs.at[0], cr.at[3], send.at[6], recv.at[6], (west, south)))
        copies.append(remote(cs.at[1], cr.at[2], send.at[7], recv.at[7], (west, north)))
        copies.append(remote(cs.at[2], cr.at[1], send.at[8], recv.at[8], (east, south)))
        copies.append(remote(cs.at[3], cr.at[0], send.at[9], recv.at[9], (east, north)))
        return copies

    corners_from = [FIRST * ROW, FIRST * ROW + WY - 1, (FIRST + WX - 1) * ROW, (FIRST + WX - 1) * ROW + WY - 1]
    corners_to = [(FIRST - 1) * ROW - 1, (FIRST - 1) * ROW + WY, (FIRST + WX) * ROW - 1, (FIRST + WX) * ROW + WY]

    def pack(field, ys, cs):
        def one(t, carry):
            for side, start in enumerate((0, WY - 2)):
                for i in range(2):
                    ys[side, t, i] = field[t, pl.ds(FIRST * ROW + start + i, WX, stride=ROW), :]
            for k in range(4):
                cs[k, pl.ds(t, 1), :] = field[t, pl.ds(corners_from[k], 1), :]
            return carry
        lax.fori_loop(0, field.shape[0], one, 0)

    has_south = (r > 0).astype(jnp.float32)
    has_north = (r < PARTS - 1).astype(jnp.float32)

    def unpack(field, yr, cr):
        def one(t, carry):
            for i in range(2):
                field[t, pl.ds(FIRST * ROW - 2 + i, WX, stride=ROW), :] = yr[0, t, i] * has_south
                field[t, pl.ds(FIRST * ROW + WY + i, WX, stride=ROW), :] = yr[1, t, i] * has_north
            for k in range(4):
                inside = has_south if k % 2 == 0 else has_north
                field[t, pl.ds(corners_to[k], 1), :] = cr[k, pl.ds(t, 1), :] * inside
            return carry
        lax.fori_loop(0, field.shape[0], one, 0)

    for x in range(WX):
        sea_ext[0, pl.ds((FIRST + x) * ROW, WY), :] = sea[pl.ds(x * WY, WY), :]
    pack(sea_ext, sysend, scsend)
    sea_copies = halo_copies(sea_ext, sysend, syrecv, scsend, screcv, sea_send, sea_recv)
    for copy in sea_copies:
        copy.start()

    for copy in own_in + entering:
        copy.wait()

    def turn(t, carry):
        for half in range(2):
            block = flat[pl.ds(pl.multiple_of(t * 128, 128), 128), half * 128:(half + 1) * 128].T
            for i in range(4):
                ext[0, t, pl.ds((FIRST + 4 * half + i) * ROW, WY), :] = block[i * WY:(i + 1) * WY]
        return carry

    lax.fori_loop(0, NT, turn, 0)

    for copy in sea_copies:
        copy.wait()
    unpack(sea_ext, syrecv, screcv)
    for copy in weights:
        copy.wait()

    def advance(cx, cy, e_at, u_at, v_at, here, size, sea_here):
        new = e_at(here, size) * (1.0 - jnp.abs(cx + u_at(here, size)) - jnp.abs(cy + v_at(here, size)))
        new += jnp.maximum(cx + u_at(here - ROW, size), 0.0) * e_at(here - ROW, size)
        new -= jnp.minimum(cx + u_at(here + ROW, size), 0.0) * e_at(here + ROW, size)
        new += jnp.maximum(cy + v_at(here - 1, size), 0.0) * e_at(here - 1, size)
        new -= jnp.minimum(cy + v_at(here + 1, size), 0.0) * e_at(here + 1, size)
        return new * sea_here

    u_at = lambda at, size: tu[pl.ds(at, size), :]
    v_at = lambda at, size: tv[pl.ds(at, size), :]

    def step_body(step, carry):
        field, after = ext.at[step], ext.at[step + 1]
        pack(field, ysend.at[step], csend.at[step])
        copies = halo_copies(
            field, ysend.at[step], yrecv.at[step], csend.at[step], crecv.at[step],
            halo_send.at[step], halo_recv.at[step])
        for copy in copies:
            copy.start()
        for copy in copies:
            copy.wait()
        unpack(field, yrecv.at[step], crecv.at[step])

        def currents(row, c):
            at = pl.multiple_of(row * ROW, 8)
            top = DOPPLER * jnp.tanh(field[OT, pl.ds(at, ROW), :])
            tu[pl.ds(at, ROW), :] = jnp.broadcast_to(top[:, 0:1], (ROW, 128))
            tv[pl.ds(at, ROW), :] = jnp.broadcast_to(top[:, 1:2], (ROW, 128))
            return c

        lax.fori_loop(1, ROWS, currents, 0)

        def first(i, c):
            at = pl.multiple_of(i * 8, 8)
            sea_here = sea_ext[0, pl.ds(at, 8), :]
            for t in range(LT):
                e1[t, pl.ds(at, 8), :] = advance(
                    cg[0, t], cg[1, t], lambda a, s: field[t, pl.ds(a, s), :], u_at, v_at, at, 8, sea_here)
            return c

        lax.fori_loop(2 * ROW // 8, 12 * ROW // 8, first, 0)

        def second(i, c):
            at = pl.multiple_of(own_row(lax.div(i, 2)) + lax.rem(i, 2) * 16, 8)
            to = pl.multiple_of(i * 16, 16)
            sea_here = sea_ext[0, pl.ds(at, 16), :]
            total = jnp.zeros((16, 128), jnp.float32)
            for t in range(LT):
                cx = jnp.concatenate([cg[0, t]] * 2, axis=0)
                cy = jnp.concatenate([cg[1, t]] * 2, axis=0)
                new = advance(cx, cy, lambda a, s: e1[t, pl.ds(a, s), :], u_at, v_at, at, 16, sea_here)
                e2[t, pl.ds(to, 16), :] = new
                square = new * new
                total += square
                rounded[pl.ds(to, 16), t * 128:(t + 1) * 128] = new.astype(jnp.bfloat16)
                squared[pl.ds(to, 16), t * 128:(t + 1) * 128] = square.astype(jnp.bfloat16)
            total = jnp.sum(total, axis=1, keepdims=True)
            scale = DT_SOURCE / (1.0 + total / NB)
            weight[pl.ds(to, 16), :] = sea_here * scale
            return c

        lax.fori_loop(0, COLS // 16, second, 0)

        drift[...] = jnp.zeros_like(drift)

        def source(first_tile, count):
            rows = pl.ds(pl.multiple_of(first_tile * 128, 128), count * 128)
            inter = lax.dot_general(rounded[...], klv[rows, :], TRANSPOSED, preferred_element_type=jnp.float32)
            inter += lax.dot_general(squared[...], ksv[rows, :], TRANSPOSED, preferred_element_type=jnp.float32)
            fresh = []
            for k in range(count):
                old = e2[first_tile + k]
                new = old + inter[:, k * 128:(k + 1) * 128] * old * weight[...]
                for x in range(WX):
                    after[first_tile + k, pl.ds((FIRST + x) * ROW, WY), :] = new[x * WY:(x + 1) * WY]
                fresh.append(new.astype(jnp.bfloat16))
            fresh = jnp.concatenate(fresh, axis=1) if count > 1 else fresh[0]
            drift[...] += lax.dot_general(fresh, dkv[:, rows], TRANSPOSED, preferred_element_type=jnp.float32)

        def pair(n, c):
            source(2 * n, 2)
            return c

        lax.fori_loop(0, LT // 2, pair, 0)
        source(LT - 1, 1)

        lane = lax.broadcasted_iota(jnp.int32, (WY, 128), 1)
        even = lax.rem(lane, 2) == 0
        sign = jnp.where(even, DT_OCEAN, -DT_OCEAN)

        def swim(x, c):
            at = own_row(x)
            old = field[OT, pl.ds(at, WY), :]
            lap = (field[OT, pl.ds(at + ROW, WY), :] + field[OT, pl.ds(at - ROW, WY), :]
                   + (field[OT, pl.ds(at + 1, WY), :] + field[OT, pl.ds(at - 1, WY), :]) - 4.0 * old)
            pushed = old + drift[pl.ds(pl.multiple_of(x * WY, WY), WY), :]
            other = jnp.where(even, pltpu.roll(pushed, 127, 1), pltpu.roll(pushed, 1, 1))
            after[OT, pl.ds(at, WY), :] = (old + (sign * other + DT_OCEAN * lap)) * sea_ext[0, pl.ds(at, WY), :]
            return c

        lax.fori_loop(0, WX, swim, 0)
        return carry

    lax.fori_loop(0, STEPS, step_body, 0)

    def turn_back(t, carry):
        for half in range(2):
            block = jnp.concatenate(
                [ext[STEPS, t, pl.ds((FIRST + 4 * half + i) * ROW, WY), :] for i in range(4)], axis=0)
            flat[pl.ds(pl.multiple_of(t * 128, 128), 128), half * 128:(half + 1) * 128] = block.T
        return carry

    lax.fori_loop(0, NT, turn_back, 0)

    def mine(peer):
        return (flat.at[pl.ds(pl.multiple_of(NB + peer * CHAN, 8), CHAN)],
                flat.at[pl.ds(pl.multiple_of(peer * BINS, 8), BINS)])

    own_o, own_e = mine(r)
    leaving = [pltpu.make_async_copy(own_o, oo.at[r], local.at[3]), pltpu.make_async_copy(own_e, eo.at[r], local.at[4])]
    for d in range(1, PARTS):
        peer = lax.rem(r + d, PARTS)
        src_o, src_e = mine(peer)
        leaving.append(remote(src_o, oo.at[r], out_send.at[0, d], out_recv.at[0, d], (g, peer)))
        leaving.append(remote(src_e, eo.at[r], out_send.at[1, d], out_recv.at[1, d], (g, peer)))
    for copy in leaving:
        copy.start()
    for copy in leaving:
        copy.wait()


def per_device(spectrum, sea_mask, kernel_linear, kernel_square, drift_kernel, ocean):
    r = lax.axis_index("bins")
    xs = spectrum.reshape(BINS, WX, PARTS, WY).transpose(2, 0, 1, 3).reshape(PARTS, BINS, COLS)
    levels = ocean.shape[1]
    os = ocean.reshape(2, levels, WX, PARTS, WY).transpose(3, 1, 0, 2, 4).reshape(PARTS, CHAN, COLS)
    sea = lax.dynamic_slice_in_dim(sea_mask.astype(jnp.float32), r * WY, WY, axis=1)
    sea = jnp.broadcast_to(sea.reshape(COLS, 1), (COLS, 128))

    any_ = pl.BlockSpec(memory_space=pl.ANY)
    vmem = pl.BlockSpec(memory_space=pltpu.VMEM)
    f32, bf16 = jnp.float32, jnp.bfloat16
    eo, oo = pl.pallas_call(
        kernel,
        out_shape=(
            jax.ShapeDtypeStruct((PARTS, BINS, COLS), f32),
            jax.ShapeDtypeStruct((PARTS, CHAN, COLS), f32),
        ),
        in_specs=[any_, any_, vmem, any_, any_, any_, vmem],
        out_specs=(any_, any_),
        scratch_shapes=[
            pltpu.VMEM((NT * 128, COLS), f32),
            pltpu.VMEM((STEPS + 1, NT, EXT, 128), f32),
            pltpu.VMEM((1, EXT, 128), f32),
            pltpu.VMEM((LT, EXT, 128), f32),
            pltpu.VMEM((LT, COLS, 128), f32),
            pltpu.VMEM((COLS, NB), bf16),
            pltpu.VMEM((COLS, NB), bf16),
            pltpu.VMEM((EXT, 128), f32),
            pltpu.VMEM((EXT, 128), f32),
            pltpu.VMEM((COLS, 128), f32),
            pltpu.VMEM((COLS, 128), f32),
            pltpu.VMEM((NB, NB), bf16),
            pltpu.VMEM((NB, NB), bf16),
            pltpu.VMEM((128, NB), bf16),
            pltpu.VMEM((STEPS, 2, NT, 2, WX, 128), f32),
            pltpu.VMEM((STEPS, 2, NT, 2, WX, 128), f32),
            pltpu.VMEM((STEPS, 4, 16, 128), f32),
            pltpu.VMEM((STEPS, 4, 16, 128), f32),
            pltpu.VMEM((2, 1, 2, WX, 128), f32),
            pltpu.VMEM((2, 1, 2, WX, 128), f32),
            pltpu.VMEM((4, 8, 128), f32),
            pltpu.VMEM((4, 8, 128), f32),
            pltpu.SemaphoreType.DMA((2, PARTS)),
            pltpu.SemaphoreType.DMA((2, PARTS)),
            pltpu.SemaphoreType.DMA((STEPS, 10)),
            pltpu.SemaphoreType.DMA((STEPS, 10)),
            pltpu.SemaphoreType.DMA((10,)),
            pltpu.SemaphoreType.DMA((10,)),
            pltpu.SemaphoreType.DMA((2, PARTS)),
            pltpu.SemaphoreType.DMA((2, PARTS)),
            pltpu.SemaphoreType.DMA((5,)),
        ],
        compiler_params=pltpu.CompilerParams(
            collective_id=0, has_side_effects=True, vmem_limit_bytes=60 * 1024 * 1024
        ),
        name="coupled",
    )(xs, os, sea, kernel_linear, kernel_square, drift_kernel, jnp.asarray(group_speeds()))
    energy = eo.reshape(PARTS, BINS, WX, WY).transpose(1, 2, 0, 3).reshape(BINS, WX, PARTS * WY)
    ocean_out = oo.reshape(PARTS, levels, 2, WX, WY).transpose(2, 1, 3, 0, 4).reshape(2, levels, WX, PARTS * WY)
    return energy, ocean_out


def solution(mesh):
    return jax.shard_map(
        per_device,
        mesh=mesh,
        in_specs=(
            P("bins", "geo", None),
            P("geo", None),
            P(),
            P(),
            P(),
            P(None, "bins", "geo", None),
        ),
        out_specs=(P("bins", "geo", None), P(None, "bins", "geo", None)),
        check_vma=False,
    )
```

time: 302 us -> 126 us (0.42); the launches traced: 297 us -> 126 us
  Pallas kernels: 0 us -> 109 us
  blocking collectives: 95 us -> 0 us
  starting transfers between devices: 73.1 us -> 0 us
  waiting for transfers between devices: 60.5 us -> 0 us
  other arithmetic: 23.3 us -> 0.76 us
  matrix products: 15.4 us -> 0 us
  local copies, waits for them, and re-layouts: 28 us -> 15.3 us
    pallas_call x0 -> x1, Pallas kernels: none -> 109 us  [per_device(): pl.pallas_call(kernel, out_shape=(jax.ShapeDtypeStruct((PARTS, BINS, COLS...]
    all_gather x3 -> x0, blocking collectives: 53.4 us -> none  [broadcast(): lax.all_gather(shard, axis)]
    all_to_all x2 -> x0, blocking collectives: 41.6 us -> none  [per_device(): lax.all_to_all(energy_flat, 'bins', split_axis=1, concat_axis=0, tiled=True)]
    ppermute x12 -> x0, starting transfers between devices: 40.6 us -> none  [the longest x6 30.8 us: extended_2(): after = lax.ppermute(first, axis, down)]
    ppermute x12 -> x0, waiting for transfers between devices: 34.1 us -> none  [the longest x6 33.3 us: extended_2(): before = lax.ppermute(last, axis, up)]
    all_to_all x7 -> x0, starting transfers between devices: 32.5 us -> none  [the longest x3 15.1 us: per_device(): lax.all_to_all(updated, 'bins', split_axis=0, concat_axis=1, tiled=True)]
    all_to_all x7 -> x0, waiting for transfers between devices: 26.5 us -> none  [the longest x1 16.4 us: per_device(): lax.all_to_all(energy_flat, 'bins', split_axis=1, concat_axis=0, tiled=True)]
    dot_general x9 -> x0, matrix products: 15.4 us -> none  [the longest x3 7.41 us: per_device(): jnp.dot(kernel_linear, rounded, preferred_element_type=jnp.float32)]
  transfers between devices with their start and end apart: 19 -> 0, of which waited for: 10 -> 0; matrix products, arithmetic and copies ran while one was open for 3% -> 0% of each run, Pallas kernels for 0% -> 0%
where the time goes in v1:
time: 126 us
  Pallas kernels  109 us (87%)
  local copies, waits for them, and re-layouts  15.3 us (12%)
    pallas_call x1, Pallas kernels, per_device(): pl.pallas_call(kernel, out_shape=(jax.ShapeDtypeStruct((PARTS, BINS, COLS...  109 us
    unnamed x6, local copies, waits for them, and re-layouts  5.5 us

profile of v1, /device:TPU:1, one launch (start us, length us, event | category | flops | bytes accessed | tf_op | source)
XLA Modules:
  0.0 125.6 jit_solution(12965872422534136792)
XLA Ops:
  0.6 0.8 dynamic-slice_convert_fusion
  1.4 0.1 broadcast_in_dim.7
  1.5 0.8 broadcast_in_dim.8.sea
  2.2 2.7 %copy.13 = f32[144,8,256]{0,2,1:T(8,128)} copy(f32[144,8,256]{2,1,0:T(8,128)} %param.7) | data formatting | bytes 2359296 | tf_op args[0]
  5.0 1.7 %copy.14 = f32[8,144,8,32]{1,3,2,0:T(8,128)S(1)} copy(f32[8,144,8,32]{1,3,0,2:T(8,128)} %bitcast.21) | data formatting | bytes 2359296 | tf_op jit(solution)/shard_map/transpose | solution.py:303
  6.7 0.0 copy-start
  6.7 1.6 %copy.16.xs = f32[8,144,256]{2,1,0:T(8,128)} copy(f32[8,144,256]{1,2,0:T(8,128)S(1)} %bitcast.18) | data formatting | bytes 2359296 | tf_op jit(solution)/shard_map/reshape | solution.py:303
  8.3 0.0 copy-done
  8.3 0.2 reshape.32
  8.5 0.1 copy.22
  8.6 0.8 reshape.33.os
  9.4 108.8 %coupled.1 = (f32[8,144,256]{2,1,0:T(8,128)}, f32[8,16,256]{2,1,0:T(8,128)}) custom-call(f32[8,144,256]{2,1,0:T(8,128)} %copy.16.xs, f32[8,16,256]{2,1,0:T(8,128)} %reshape.33.os, f32[256,128]{1,0:T(8,128)} %broadcast_in_dim.8.sea, bf16[1152,1152]{1,0:T(8,128)(2,1)} %kl.1, bf16[1152,1152]{1,0:T(8,128)(2,1)} %ks.1, bf16[128,1152]{1,0:T(8,128)(2,1)} %dk.1, ...), custom_call_target="tpu_custom_call" | custom-call | tf_op jit(solution)/shard_map/coupled/pallas_call | solution.py:312
  118.2 1.8 %copy.17 = f32[8,144,256]{1,2,0:T(8,128)S(1)} copy(f32[8,144,256]{2,1,0:T(8,128)} %get-tuple-element.4) | data formatting | bytes 2359296 | tf_op jit(solution)/shard_map/coupled/pallas_call | solution.py:312
  120.0 1.5 %copy.18 = f32[144,8,8,32]{0,3,2,1:T(8,128)} copy(f32[144,8,8,32]{0,3,1,2:T(8,128)S(1)} %bitcast.19) | data formatting | bytes 2359296 | tf_op jit(solution)/shard_map/transpose | solution.py:358
  121.5 0.0 copy-start.1
  121.5 2.8 %copy.20 = f32[144,8,256]{2,1,0:T(8,128)} copy(f32[144,8,256]{0,2,1:T(8,128)} %bitcast.20) | data formatting | bytes 2359296
  124.2 0.0 copy-done.1
  124.2 0.2 reshape.36
  124.4 0.3 copy.19
  124.7 0.8 reshape.37
Async XLA Ops:
  6.7 1.6 %copy-start = (f32[2,8,8,256]{3,2,1,0:T(8,128)S(1)}, f32[2,8,8,256]{3,2,1,0:T(8,128)}, u32[]{:S(2)}) copy-start(f32[2,8,8,256]{3,2,1,0:T(8,128)} %param.12) | copy-start | bytes 393220
  121.5 2.8 %copy-start.1 = (f32[8,16,256]{2,1,0:T(8,128)S(1)}, f32[8,16,256]{2,1,0:T(8,128)}, u32[]{:S(2)}) copy-start(f32[8,16,256]{2,1,0:T(8,128)} %get-tuple-element.5) | copy-start | bytes 393220

commit v2 on v1

v2 whole, which is shorter than its diff:
```python
import jax
import jax.numpy as jnp
import numpy as np
from jax import lax
from jax.experimental import pallas as pl
from jax.experimental.pallas import tpu as pltpu
from jax.sharding import PartitionSpec as P

NDIR = 36
NFREQ = 32
NB = 1152
STEPS = 3
PARTS = 8
BINS = NB // PARTS
SHARE = 16
WX = 8
WY = 32
COLS = WX * WY
LT = NB // 128
OT = LT
NT = LT + 1
GROUPS = LT // 2 + 2
ROW = 40
ROWS = 13
EXT = ROW * ROWS
FIRST = 3
HOLD = 3

DT_SOURCE = 0.5
DT_OCEAN = 0.2
DOPPLER = 0.1

MESH = pl.DeviceIdType.MESH


def bin_order():
    return np.arange(NB).reshape(PARTS, LT, SHARE).transpose(1, 0, 2).reshape(NB)


def group_speeds():
    index = bin_order()
    direction = (index // NFREQ).astype(np.float32)
    frequency = (index % NFREQ).astype(np.float32)
    speed = np.float32(0.4) / (np.float32(1.0) + frequency / np.float32(16.0))
    angle = np.float32(2.0 * np.pi / NDIR) * direction
    both = np.stack([speed * np.cos(angle), speed * np.sin(angle)]).astype(np.float32)
    return np.ascontiguousarray(np.broadcast_to(both.reshape(2, LT, 1, 128), (2, LT, 8, 128)))


def own_row(x):
    return pl.multiple_of((FIRST + x) * ROW, 8)


def tile_rows(t):
    return pl.ds(pl.multiple_of(t * 128, 128), 128)


def share_rows(k):
    return pl.ds(pl.multiple_of(k * SHARE, SHARE), SHARE)


def kernel(
    spectrum, ocean, sea, kl, ks, dk, cg, eo, oo,
    spec, swim_in, send, flat, ext, sea_raw, sea_turned, sea_ext, e1, e2, rounded, squared, tu, tv, total, weight,
    drift, kl_raw, ks_raw, dk_raw, wl, ws, wd, ysend, yrecv, csend, crecv, back, got, spec_out, swim_out,
    in_send, in_recv, halo_send, halo_recv, sea_send, sea_recv, out_send, out_recv, load, weights_sem, store,
):
    g = lax.axis_index("geo")
    r = lax.axis_index("bins")
    tiles = lax.axis_size("geo")
    west, east = lax.rem(g + tiles - 1, tiles), lax.rem(g + 1, tiles)
    south, north = lax.rem(r + PARTS - 1, PARTS), lax.rem(r + 1, PARTS)

    barrier = pltpu.get_barrier_semaphore()
    friends = [(g, lax.rem(r + d, PARTS)) for d in range(1, PARTS)]
    friends += [(x, y) for x in (west, east) for y in (south, r, north)]
    for friend in friends:
        pl.semaphore_signal(barrier, inc=1, device_id=friend, device_id_type=MESH)

    def half_lanes(h):
        return pl.ds(h * 128, 128)

    loads = []
    for h in range(2):
        loads.append(pltpu.make_async_copy(ocean.at[:, half_lanes(h)], swim_in.at[h], load.at[LT, h]))

    def spec_load(t, h):
        return pltpu.make_async_copy(spectrum.at[tile_rows(t), half_lanes(h)], spec.at[h, tile_rows(t)], load.at[t, h])

    for copy in loads:
        copy.start()
    for t in range(LT):
        for h in range(2):
            spec_load(t, h).start()
    weights = [pltpu.make_async_copy(dk, dk_raw, weights_sem.at[0])]
    for t in range(LT):
        weights.append(pltpu.make_async_copy(kl.at[:, t], kl_raw.at[t], weights_sem.at[1 + t]))
        weights.append(pltpu.make_async_copy(ks.at[:, t], ks_raw.at[t], weights_sem.at[1 + LT + t]))
    for copy in weights:
        copy.start()

    lane = lax.broadcasted_iota(jnp.int32, (8, 128), 1)
    low_half = lane < 64
    even_block = lax.rem(lax.div(lane, 32), 2) == 0

    def swap_blocks(a):
        c = [None] * 4
        for i in range(2):
            c[i] = jnp.where(low_half, a[i], pltpu.roll(a[i + 2], 64, 1))
            c[i + 2] = jnp.where(low_half, pltpu.roll(a[i], 64, 1), a[i + 2])
        out = []
        for i in (0, 2):
            out.append(jnp.where(even_block, c[i], pltpu.roll(c[i + 1], 32, 1)))
            out.append(jnp.where(even_block, pltpu.roll(c[i], 96, 1), c[i + 1]))
        return out

    def remote(src, dst, send_sem, recv_sem, device):
        return pltpu.make_async_remote_copy(
            src_ref=src, dst_ref=dst, send_sem=send_sem, recv_sem=recv_sem, device_id=device, device_id_type=MESH
        )

    def entry_copies(t):
        copies = []
        for d in range(1, PARTS):
            peer = lax.rem(r + d, PARTS)
            copies.append(remote(
                send.at[t, peer], flat.at[t, :, share_rows(r)], in_send.at[t, d], in_recv.at[t, d], (g, peer)))
        return copies

    def exit_copies(t):
        copies = []
        for d in range(1, PARTS):
            peer = lax.rem(r + d, PARTS)
            copies.append(remote(
                back.at[t, :, share_rows(peer)], got.at[t, r], out_send.at[t, d], out_recv.at[t, d], (g, peer)))
        return copies

    def ship(t):
        for copy in entry_copies(t):
            copy.start()
        for half in range(2):
            flat[t, half, share_rows(r), :] = send[t, r, half]

    sea_raw[1] = sea[...].astype(jnp.float32)
    sea_copies = [
        remote(sea_raw.at[1], sea_raw.at[2], sea_send.at[0], sea_recv.at[0], (west, r)),
        remote(sea_raw.at[1], sea_raw.at[0], sea_send.at[1], sea_recv.at[1], (east, r)),
    ]

    for copy in loads:
        copy.wait()
    for comp in range(2):
        for h in range(2):
            for half in range(2):
                blocks = swap_blocks(
                    [swim_in[h, pl.ds(64 * comp + 4 * half + i, 8, stride=8), :] for i in range(4)])
                for j in range(4):
                    send[OT, 4 * h + j, half, pl.ds(comp, 8, stride=2), :] = blocks[j]

    pl.semaphore_wait(barrier, len(friends))
    for copy in sea_copies:
        copy.start()
    ship(OT)

    def enter(t, carry):
        for h in range(2):
            spec_load(t, h).wait()
        for octet in range(2):
            for h in range(2):
                for half in range(2):
                    blocks = swap_blocks([
                        spec[h, pl.ds(t * 128 + octet * 64 + 4 * half + i, 8, stride=8), :] for i in range(4)])
                    for j in range(4):
                        send[t, 4 * h + j, half, pl.ds(octet * 8, 8), :] = blocks[j]
        ship(t)
        return carry

    lax.fori_loop(0, LT, enter, 0)

    def halo_copies(step, group, first_tile, count):
        field = ext.at[step]
        every = pl.ds(first_tile, count)
        sems, semr = halo_send.at[step, group], halo_recv.at[step, group]
        ys, yr = ysend.at[step, group], yrecv.at[step, group]
        cs, cr = csend.at[step, group], crecv.at[step, group]
        some = pl.ds(0, count)
        copies = [
            remote(ys.at[0, some], yr.at[1, some], sems.at[4], semr.at[4], (g, south)),
            remote(ys.at[1, some], yr.at[0, some], sems.at[5], semr.at[5], (g, north)),
            remote(cs.at[0], cr.at[3], sems.at[6], semr.at[6], (west, south)),
            remote(cs.at[1], cr.at[2], sems.at[7], semr.at[7], (west, north)),
            remote(cs.at[2], cr.at[1], sems.at[8], semr.at[8], (east, south)),
            remote(cs.at[3], cr.at[0], sems.at[9], semr.at[9], (east, north)),
        ]
        for i in range(2):
            copies.append(remote(
                field.at[every, pl.ds((FIRST + i) * ROW, WY)],
                field.at[every, pl.ds((FIRST + WX + i) * ROW, WY)],
                sems.at[i], semr.at[i], (west, r)))
            copies.append(remote(
                field.at[every, pl.ds((FIRST + WX - 2 + i) * ROW, WY)],
                field.at[every, pl.ds((FIRST - 2 + i) * ROW, WY)],
                sems.at[2 + i], semr.at[2 + i], (east, r)))
        return copies

    corners_from = [FIRST * ROW, FIRST * ROW + WY - 1, (FIRST + WX - 1) * ROW, (FIRST + WX - 1) * ROW + WY - 1]
    corners_to = [(FIRST - 1) * ROW - 1, (FIRST - 1) * ROW + WY, (FIRST + WX) * ROW - 1, (FIRST + WX) * ROW + WY]
    has_south = (r > 0).astype(jnp.float32)
    has_north = (r < PARTS - 1).astype(jnp.float32)

    def send_halo(step, group, first_tile, count):
        for n in range(count):
            t = first_tile + n
            for side, start in enumerate((0, WY - 2)):
                for i in range(2):
                    ysend[step, group, side, n, i] = ext[step, t, pl.ds(FIRST * ROW + start + i, WX, stride=ROW), :]
            for k in range(4):
                csend[step, group, k, pl.ds(n, 1), :] = ext[step, t, pl.ds(corners_from[k], 1), :]
        for copy in halo_copies(step, group, first_tile, count):
            copy.start()

    def take_halo(step, group, first_tile, count):
        for copy in halo_copies(step, group, first_tile, count):
            copy.wait()
        for n in range(count):
            t = first_tile + n
            for i in range(2):
                ext[step, t, pl.ds(FIRST * ROW - 2 + i, WX, stride=ROW), :] = yrecv[step, group, 0, n, i] * has_south
                ext[step, t, pl.ds(FIRST * ROW + WY + i, WX, stride=ROW), :] = yrecv[step, group, 1, n, i] * has_north
            for k in range(4):
                inside = has_south if k % 2 == 0 else has_north
                ext[step, t, pl.ds(corners_to[k], 1), :] = crecv[step, group, k, pl.ds(n, 1), :] * inside

    def turn(t):
        for copy in entry_copies(t):
            copy.wait()
        for half in range(2):
            block = flat[t, half].T
            for i in range(4):
                ext[0, t, pl.ds((FIRST + 4 * half + i) * ROW, WY), :] = block[i * WY:(i + 1) * WY]

    def currents(step):
        def one(row, c):
            at = pl.multiple_of(row * ROW, 8)
            top = DOPPLER * jnp.tanh(ext[step, OT, pl.ds(at, ROW), :])
            tu[pl.ds(at, ROW), :] = jnp.broadcast_to(top[:, 0:1], (ROW, 128))
            tv[pl.ds(at, ROW), :] = jnp.broadcast_to(top[:, 1:2], (ROW, 128))
            return c
        lax.fori_loop(1, ROWS, one, 0)

    u_at = lambda at: tu[pl.ds(at, 16), :]
    v_at = lambda at: tv[pl.ds(at, 16), :]

    def advance(cx, cy, e_at, here, sea_here):
        new = e_at(here) * (1.0 - jnp.abs(cx + u_at(here)) - jnp.abs(cy + v_at(here)))
        new += jnp.maximum(cx + u_at(here - ROW), 0.0) * e_at(here - ROW)
        new -= jnp.minimum(cx + u_at(here + ROW), 0.0) * e_at(here + ROW)
        new += jnp.maximum(cy + v_at(here - 1), 0.0) * e_at(here - 1)
        new -= jnp.minimum(cy + v_at(here + 1), 0.0) * e_at(here + 1)
        return new * sea_here

    def advect(step, first_tile, count):
        def speeds(t):
            return jnp.concatenate([cg[0, t]] * 2, axis=0), jnp.concatenate([cg[1, t]] * 2, axis=0)

        def first(i, c):
            at = pl.multiple_of(i * 16, 16)
            sea_here = sea_ext[pl.ds(at, 16), :]
            for n in range(count):
                t = first_tile + n
                cx, cy = speeds(t)
                e1[t, pl.ds(at, 16), :] = advance(cx, cy, lambda a: ext[step, t, pl.ds(a, 16), :], at, sea_here)
            return c

        lax.fori_loop(2 * ROW // 16, 12 * ROW // 16, first, 0)

        def second(i, c):
            at = pl.multiple_of(own_row(lax.div(i, 2)) + lax.rem(i, 2) * 16, 8)
            to = pl.ds(pl.multiple_of(i * 16, 16), 16)
            sea_here = sea_ext[pl.ds(at, 16), :]
            squares = total[to, :]
            for n in range(count):
                t = first_tile + n
                cx, cy = speeds(t)
                new = advance(cx, cy, lambda a: e1[t, pl.ds(a, 16), :], at, sea_here)
                e2[t, to, :] = new
                square = new * new
                squares += square
                rounded[to, tile_rows(t)] = new.astype(jnp.bfloat16)
                squared[to, tile_rows(t)] = square.astype(jnp.bfloat16)
            total[to, :] = squares
            return c

        lax.fori_loop(0, COLS // 16, second, 0)

    def weigh():
        def one(x, c):
            to = pl.ds(pl.multiple_of(x * WY, WY), WY)
            sums = jnp.sum(total[to, :], axis=1, keepdims=True)
            weight[to, :] = sea_ext[pl.ds(own_row(x), WY), :] * (DT_SOURCE / (1.0 + sums / NB))
            return c
        lax.fori_loop(0, WX, one, 0)

    def prepare(v):
        for raw, out in ((kl_raw, wl), (ks_raw, ws)):
            for u in range(LT):
                block = raw[v].reshape(128, NB)[:, u * 128:(u + 1) * 128].T
                for i in range(8):
                    k, t = divmod(8 * u + i, LT)
                    out[pl.ds(128 * t + SHARE * k, SHARE), tile_rows(v)] = block[i * SHARE:(i + 1) * SHARE]

    turn(OT)
    send_halo(0, GROUPS - 1, OT, 1)

    for copy in sea_copies:
        copy.wait()
    sea_turned[...] = jnp.zeros_like(sea_turned)
    for h in range(2):
        lanes = slice(h * 128, (h + 1) * 128)
        rows = jnp.concatenate(
            [sea_raw[0, :, lanes], sea_raw[1, :, lanes], sea_raw[2, :, lanes], jnp.zeros((104, 128), jnp.float32)], axis=0)
        sea_turned[pl.ds(8 + h * 128, 128), :] = rows.T
    for q in range(12):
        column = q + 6
        here = sea_turned[pl.ds(pl.multiple_of(8 + r * WY, 8), ROW), :]
        sea_ext[pl.ds((q + 1) * ROW, ROW), :] = jnp.broadcast_to(here[:, column:column + 1], (ROW, 128))
        left = sea_turned[pl.ds(6 + r * WY, 2), :]
        sea_ext[pl.ds((q + 1) * ROW - 2, 2), :] = jnp.broadcast_to(left[:, column:column + 1], (2, 128))

    for copy in weights:
        copy.wait()
    for u in range(LT):
        block = dk_raw[:, u * 128:(u + 1) * 128].T
        for i in range(8):
            k, t = divmod(8 * u + i, LT)
            wd[pl.ds(128 * t + SHARE * k, SHARE), :] = block[i * SHARE:(i + 1) * SHARE]

    take_halo(0, GROUPS - 1, OT, 1)
    currents(0)
    total[...] = jnp.zeros_like(total)

    def enter_pair(n, c):
        turn(2 * n)
        turn(2 * n + 1)
        send_halo(0, n, 2 * n, 2)
        prepare(2 * n)
        prepare(2 * n + 1)

        @pl.when(n > 0)
        def _():
            take_halo(0, n - 1, 2 * n - 2, 2)
            advect(0, 2 * n - 2, 2)

        return c

    lax.fori_loop(0, LT // 2, enter_pair, 0)
    turn(LT - 1)
    send_halo(0, GROUPS - 2, LT - 1, 1)
    prepare(LT - 1)
    take_halo(0, GROUPS - 3, LT - 3, 2)
    advect(0, LT - 3, 2)
    take_halo(0, GROUPS - 2, LT - 1, 1)
    advect(0, LT - 1, 1)

    lane_row = lax.broadcasted_iota(jnp.int32, (WY, 128), 1)
    even = lax.rem(lane_row, 2) == 0
    sign = jnp.where(even, DT_OCEAN, -DT_OCEAN)

    def turn_back(t, value):
        for half in range(2):
            back[t, half] = value[half * 128:(half + 1) * 128].T
        for copy in exit_copies(t):
            copy.start()
        for half in range(2):
            got[t, r, half] = back[t, half, share_rows(r), :]

    def source(step, first_tile, count, group, now):
        lanes = pl.ds(pl.multiple_of(first_tile * 128, 128), count * 128)
        inter = jnp.dot(rounded[...], wl[:, lanes], preferred_element_type=jnp.float32)
        inter += jnp.dot(squared[...], ws[:, lanes], preferred_element_type=jnp.float32)
        fresh = []
        for k in range(count):
            old = e2[first_tile + k]
            new = old + inter[:, k * 128:(k + 1) * 128] * old * weight[...]
            if step < STEPS - 1:
                for x in range(WX):
                    ext[step + 1, first_tile + k, pl.ds((FIRST + x) * ROW, WY), :] = new[x * WY:(x + 1) * WY]
            else:
                turn_back(first_tile + k, new)
            fresh.append(new.astype(jnp.bfloat16))
        fresh = jnp.concatenate(fresh, axis=1) if count > 1 else fresh[0]
        drift[...] += jnp.dot(fresh, wd[lanes, :], preferred_element_type=jnp.float32)
        if step < STEPS - 1 and now is not None:
            @pl.when(now)
            def _():
                send_halo(step + 1, group, first_tile, count)

    def swim(step):
        def one(x, c):
            at = own_row(x)
            old = ext[step, OT, pl.ds(at, WY), :]
            lap = (ext[step, OT, pl.ds(at + ROW, WY), :] + ext[step, OT, pl.ds(at - ROW, WY), :]
                   + (ext[step, OT, pl.ds(at + 1, WY), :] + ext[step, OT, pl.ds(at - 1, WY), :]) - 4.0 * old)
            here = pl.ds(pl.multiple_of(x * WY, WY), WY)
            pushed = old + drift[here, :]
            other = jnp.where(even, pltpu.roll(pushed, 127, 1), pltpu.roll(pushed, 1, 1))
            new = (old + (sign * other + DT_OCEAN * lap)) * sea_ext[pl.ds(at, WY), :]
            if step < STEPS - 1:
                ext[step + 1, OT, pl.ds(at, WY), :] = new
            else:
                drift[here, :] = new
            return c
        lax.fori_loop(0, WX, one, 0)
        if step == STEPS - 1:
            turn_back(OT, drift[...])

    for step in range(STEPS):
        if step:
            take_halo(step, GROUPS - 1, OT, 1)
            currents(step)
            total[...] = jnp.zeros_like(total)

            def advect_pair(n, c):
                take_halo(step, n, 2 * n, 2)
                advect(step, 2 * n, 2)
                return c

            lax.fori_loop(0, LT // 2, advect_pair, 0)
            take_halo(step, GROUPS - 2, LT - 1, 1)
            advect(step, LT - 1, 1)
        weigh()
        drift[...] = jnp.zeros_like(drift)

        def source_pair(n, c):
            source(step, 2 * n, 2, n, n < HOLD)
            return c

        lax.fori_loop(0, LT // 2, source_pair, 0)
        source(step, LT - 1, 1, None, None)
        swim(step)
        if step < STEPS - 1:
            send_halo(step + 1, GROUPS - 1, OT, 1)
            for n in range(HOLD, LT // 2):
                send_halo(step + 1, n, 2 * n, 2)
            send_halo(step + 1, GROUPS - 2, LT - 1, 1)

    def spec_store(t, h):
        return pltpu.make_async_copy(spec_out.at[h, tile_rows(t)], eo.at[tile_rows(t), half_lanes(h)], store.at[t, h])

    def leave(t, carry):
        for copy in exit_copies(t):
            copy.wait()
        for octet in range(2):
            for h in range(2):
                for half in range(2):
                    blocks = swap_blocks([got[t, 4 * h + j, half, pl.ds(octet * 8, 8), :] for j in range(4)])
                    for i in range(4):
                        spec_out[h, pl.ds(t * 128 + octet * 64 + 4 * half + i, 8, stride=8), :] = blocks[i]
        for h in range(2):
            spec_store(t, h).start()
        return carry

    lax.fori_loop(0, LT, leave, 0)
    for copy in exit_copies(OT):
        copy.wait()
    for comp in range(2):
        for h in range(2):
            for half in range(2):
                blocks = swap_blocks([got[OT, 4 * h + j, half, pl.ds(comp, 8, stride=2), :] for j in range(4)])
                for i in range(4):
                    swim_out[h, pl.ds(64 * comp + 4 * half + i, 8, stride=8), :] = blocks[i]
    stores = [pltpu.make_async_copy(swim_out.at[h], oo.at[:, half_lanes(h)], store.at[LT, h]) for h in range(2)]
    for copy in stores:
        copy.start()
    for t in range(LT):
        for h in range(2):
            spec_store(t, h).wait()
    for copy in stores:
        copy.wait()


def per_device(spectrum, sea_mask, kernel_linear, kernel_square, drift_kernel, ocean):
    y = spectrum.shape[2]
    any_ = pl.BlockSpec(memory_space=pl.ANY)
    vmem = pl.BlockSpec(memory_space=pltpu.VMEM)
    f32, bf16 = jnp.float32, jnp.bfloat16
    dma = pltpu.SemaphoreType.DMA
    eo, oo = pl.pallas_call(
        kernel,
        out_shape=(jax.ShapeDtypeStruct((NB, y), f32), jax.ShapeDtypeStruct((128, y), f32)),
        in_specs=[any_, any_, vmem, any_, any_, any_, vmem],
        out_specs=(any_, any_),
        scratch_shapes=[
            pltpu.VMEM((2, NB, 128), f32),
            pltpu.VMEM((2, 128, 128), f32),
            pltpu.VMEM((NT, PARTS, 2, SHARE, 128), f32),
            pltpu.VMEM((NT, 2, 128, 128), f32),
            pltpu.VMEM((STEPS, NT, EXT, 128), f32),
            pltpu.VMEM((3, 8, y), f32),
            pltpu.VMEM((8 + 256 + ROW, 128), f32),
            pltpu.VMEM((EXT, 128), f32),
            pltpu.VMEM((LT, EXT, 128), f32),
            pltpu.VMEM((LT, COLS, 128), f32),
            pltpu.VMEM((COLS, NB), bf16),
            pltpu.VMEM((COLS, NB), bf16),
            pltpu.VMEM((EXT, 128), f32),
            pltpu.VMEM((EXT, 128), f32),
            pltpu.VMEM((COLS, 128), f32),
            pltpu.VMEM((COLS, 128), f32),
            pltpu.VMEM((COLS, 128), f32),
            pltpu.VMEM((LT, PARTS, SHARE, NB), bf16),
            pltpu.VMEM((LT, PARTS, SHARE, NB), bf16),
            pltpu.VMEM((128, NB), bf16),
            pltpu.VMEM((NB, NB), bf16),
            pltpu.VMEM((NB, NB), bf16),
            pltpu.VMEM((NB, 128), bf16),
            pltpu.VMEM((STEPS, GROUPS, 2, 2, 2, WX, 128), f32),
            pltpu.VMEM((STEPS, GROUPS, 2, 2, 2, WX, 128), f32),
            pltpu.VMEM((STEPS, GROUPS, 4, 8, 128), f32),
            pltpu.VMEM((STEPS, GROUPS, 4, 8, 128), f32),
            pltpu.VMEM((NT, 2, 128, 128), f32),
            pltpu.VMEM((NT, PARTS, 2, SHARE, 128), f32),
            pltpu.VMEM((2, NB, 128), f32),
            pltpu.VMEM((2, 128, 128), f32),
            dma((NT, PARTS)),
            dma((NT, PARTS)),
            dma((STEPS, GROUPS, 10)),
            dma((STEPS, GROUPS, 10)),
            dma((2,)),
            dma((2,)),
            dma((NT, PARTS)),
            dma((NT, PARTS)),
            dma((NT, 2)),
            dma((1 + 2 * LT,)),
            dma((NT, 2)),
        ],
        compiler_params=pltpu.CompilerParams(
            collective_id=0, has_side_effects=True, vmem_limit_bytes=60 * 1024 * 1024
        ),
        name="coupled",
    )(
        spectrum.reshape(NB, y),
        ocean.reshape(128, y),
        sea_mask,
        kernel_linear.reshape(PARTS, LT, SHARE, NB),
        kernel_square.reshape(PARTS, LT, SHARE, NB),
        drift_kernel,
        jnp.asarray(group_speeds()),
    )
    return eo.reshape(spectrum.shape), oo.reshape(ocean.shape)


def solution(mesh):
    return jax.shard_map(
        per_device,
        mesh=mesh,
        in_specs=(
            P("bins", "geo", None),
            P("geo", None),
            P(),
            P(),
            P(),
            P(None, "bins", "geo", None),
        ),
        out_specs=(P("bins", "geo", None), P(None, "bins", "geo", None)),
        check_vma=False,
    )
```

time: 126 us -> 110 us (0.87)
  local copies, waits for them, and re-layouts: 15.3 us -> 3.05 us
  Pallas kernels: 109 us -> 106 us
    reshape x6 -> x0, local copies, waits for them, and re-layouts: 3.71 us -> none  [the longest x1 1.6 us: per_device(): spectrum.reshape(BINS, WX, PARTS, WY).transpose(2, 0, 1, 3)]
    transpose x3 -> x0, local copies, waits for them, and re-layouts: 3.52 us -> none  [the longest x1 1.73 us: per_device(): spectrum.reshape(BINS, WX, PARTS, WY).transpose(2, 0, 1, 3)]
    pallas_call x1, Pallas kernels: 109 us -> 106 us  [per_device(): pl.pallas_call(kernel, out_shape=(jax.ShapeDtypeStruct((NB, y), f32), jax...]
    unnamed x6 -> x4, local copies, waits for them, and re-layouts: 5.5 us -> 3.05 us
    pallas_call x1 -> x0, local copies, waits for them, and re-layouts: 1.76 us -> none  [per_device(): pl.pallas_call(kernel, out_shape=(jax.ShapeDtypeStruct((PARTS, BINS, COLS...]
where the time goes in v2:
time: 110 us; the launch traced here: 109 us
  Pallas kernels  106 us (96%)
  local copies, waits for them, and re-layouts  3.05 us (3%)
    pallas_call x1, Pallas kernels, per_device(): pl.pallas_call(kernel, out_shape=(jax.ShapeDtypeStruct((NB, y), f32), jax...  106 us
    unnamed x4, local copies, waits for them, and re-layouts  3.05 us

profile of v2, /device:TPU:1, one launch (start us, length us, event | category | flops | bytes accessed | tf_op | source)
XLA Modules:
  0.0 109.4 jit_solution(4740009855953795179)
XLA Ops:
  0.6 105.7 %coupled.1 = (f32[1152,256]{1,0:T(8,128)}, f32[128,256]{1,0:T(8,128)}) custom-call(f32[1152,256]{1,0:T(8,128)} %bitcast.9, f32[128,256]{1,0:T(8,128)} %bitcast.10, s32[8,256]{1,0:T(8,128)} %sea.1, bf16[8,9,16,1152]{3,2,1,0:T(8,128)(2,1)} %bitcast.6, bf16[8,9,16,1152]{3,2,1,0:T(8,128)(2,1)} %bitcast.7, bf16[128,1152]{1,0:T(8,128)(2,1)} %dk.1, ...), custom_call_target="tpu_custom_call" | custom-call | tf_op jit(solution)/shard_map/coupled/pallas_call | solution.py:488
  106.3 0.0 copy-start
  106.3 2.4 %copy.11 = f32[144,8,256]{2,1,0:T(8,128)} copy(f32[144,8,256]{2,1,0:T(8,128)} %bitcast.8) | data formatting | bytes 2359296
  108.7 0.0 copy-done
  108.7 0.7 copy.12
Async XLA Ops:
  106.3 2.4 %copy-start = (f32[128,256]{1,0:T(8,128)S(1)}, f32[128,256]{1,0:T(8,128)}, u32[]{:S(2)}) copy-start(f32[128,256]{1,0:T(8,128)} %get-tuple-element.5) | copy-start | bytes 393220

commit v3 on v2

--- a/solution.py
+++ b/solution.py
@@ -19,12 +19,12 @@
 LT = NB // 128
 OT = LT
 NT = LT + 1
-GROUPS = LT // 2 + 2
+GROUPS = ((0, 4), (4, 4), (8, 1), (OT, 1))
+SMALL = WX * 2
 ROW = 40
 ROWS = 13
 EXT = ROW * ROWS
 FIRST = 3
-HOLD = 3
 
 DT_SOURCE = 0.5
 DT_OCEAN = 0.2
@@ -80,24 +80,18 @@
     def half_lanes(h):
         return pl.ds(h * 128, 128)
 
-    loads = []
+    def drain(sem, rows):
+        pltpu.make_async_copy(e1.at[pl.ds(0, rows)], e1.at[pl.ds(0, rows)], sem).wait()
+
+    def spec_load(t, c):
+        for h in range(2):
+            pltpu.make_async_copy(
+                spectrum.at[tile_rows(t), half_lanes(h)], spec.at[h, tile_rows(t)], load.at[t]).start()
+        return c
+
     for h in range(2):
-        loads.append(pltpu.make_async_copy(ocean.at[:, half_lanes(h)], swim_in.at[h], load.at[LT, h]))
-
-    def spec_load(t, h):
-        return pltpu.make_async_copy(spectrum.at[tile_rows(t), half_lanes(h)], spec.at[h, tile_rows(t)], load.at[t, h])
-
-    for copy in loads:
-        copy.start()
-    for t in range(LT):
-        for h in range(2):
-            spec_load(t, h).start()
-    weights = [pltpu.make_async_copy(dk, dk_raw, weights_sem.at[0])]
-    for t in range(LT):
-        weights.append(pltpu.make_async_copy(kl.at[:, t], kl_raw.at[t], weights_sem.at[1 + t]))
-        weights.append(pltpu.make_async_copy(ks.at[:, t], ks_raw.at[t], weights_sem.at[1 + LT + t]))
-    for copy in weights:
-        copy.start()
+        pltpu.make_async_copy(ocean.at[:, half_lanes(h)], swim_in.at[h], load.at[LT]).start()
+    lax.fori_loop(0, LT, spec_load, 0)
 
     lane = lax.broadcasted_iota(jnp.int32, (8, 128), 1)
     low_half = lane < 64
@@ -124,7 +118,7 @@
         for d in range(1, PARTS):
             peer = lax.rem(r + d, PARTS)
             copies.append(remote(
-                send.at[t, peer], flat.at[t, :, share_rows(r)], in_send.at[t, d], in_recv.at[t, d], (g, peer)))
+                send.at[t, peer], flat.at[t, :, share_rows(r)], in_send.at[0], in_recv.at[t], (g, peer)))
         return copies
 
     def exit_copies(t):
@@ -132,7 +126,7 @@
         for d in range(1, PARTS):
             peer = lax.rem(r + d, PARTS)
             copies.append(remote(
-                back.at[t, :, share_rows(peer)], got.at[t, r], out_send.at[t, d], out_recv.at[t, d], (g, peer)))
+                back.at[t, :, share_rows(peer)], got.at[t, r], out_send.at[0], out_recv.at[t], (g, peer)))
         return copies
 
     def ship(t):
@@ -144,11 +138,10 @@
     sea_raw[1] = sea[...].astype(jnp.float32)
     sea_copies = [
         remote(sea_raw.at[1], sea_raw.at[2], sea_send.at[0], sea_recv.at[0], (west, r)),
-        remote(sea_raw.at[1], sea_raw.at[0], sea_send.at[1], sea_recv.at[1], (east, r)),
+        remote(sea_raw.at[1], sea_raw.at[0], sea_send.at[0], sea_recv.at[0], (east, r)),
     ]
 
-    for copy in loads:
-        copy.wait()
+    drain(load.at[LT], 256)
     for comp in range(2):
         for h in range(2):
             for half in range(2):
@@ -163,8 +156,7 @@
     ship(OT)
 
     def enter(t, carry):
-        for h in range(2):
-            spec_load(t, h).wait()
+        drain(load.at[t], 256)
         for octet in range(2):
             for h in range(2):
                 for half in range(2):
@@ -177,30 +169,38 @@
 
     lax.fori_loop(0, LT, enter, 0)
 
-    def halo_copies(step, group, first_tile, count):
+    def weights_load(t, c):
+        pltpu.make_async_copy(kl.at[:, t], kl_raw.at[t], weights_sem.at[1]).start()
+        pltpu.make_async_copy(ks.at[:, t], ks_raw.at[t], weights_sem.at[2]).start()
+        return c
+
+    pltpu.make_async_copy(dk, dk_raw, weights_sem.at[0]).start()
+    lax.fori_loop(0, LT, weights_load, 0)
+
+    def halo_copies(step, group):
+        first_tile, count = GROUPS[group]
         field = ext.at[step]
         every = pl.ds(first_tile, count)
-        sems, semr = halo_send.at[step, group], halo_recv.at[step, group]
-        ys, yr = ysend.at[step, group], yrecv.at[step, group]
+        sems, semr = halo_send.at[step], halo_recv.at[step, group]
+        ys, yr = ysend.at[step], yrecv.at[step]
         cs, cr = csend.at[step, group], crecv.at[step, group]
-        some = pl.ds(0, count)
         copies = [
-            remote(ys.at[0, some], yr.at[1, some], sems.at[4], semr.at[4], (g, south)),
-            remote(ys.at[1, some], yr.at[0, some], sems.at[5], semr.at[5], (g, north)),
-            remote(cs.at[0], cr.at[3], sems.at[6], semr.at[6], (west, south)),
-            remote(cs.at[1], cr.at[2], sems.at[7], semr.at[7], (west, north)),
-            remote(cs.at[2], cr.at[1], sems.at[8], semr.at[8], (east, south)),
-            remote(cs.at[3], cr.at[0], sems.at[9], semr.at[9], (east, north)),
+            remote(ys.at[0, every], yr.at[1, every], sems, semr, (g, south)),
+            remote(ys.at[1, every], yr.at[0, every], sems, semr, (g, north)),
+            remote(cs.at[0], cr.at[3], sems, semr, (west, south)),
+            remote(cs.at[1], cr.at[2], sems, semr, (west, north)),
+            remote(cs.at[2], cr.at[1], sems, semr, (east, south)),
+            remote(cs.at[3], cr.at[0], sems, semr, (east, north)),
         ]
         for i in range(2):
             copies.append(remote(
                 field.at[every, pl.ds((FIRST + i) * ROW, WY)],
                 field.at[every, pl.ds((FIRST + WX + i) * ROW, WY)],
-                sems.at[i], semr.at[i], (west, r)))
+                sems, semr, (west, r)))
             copies.append(remote(
                 field.at[every, pl.ds((FIRST + WX - 2 + i) * ROW, WY)],
                 field.at[every, pl.ds((FIRST - 2 + i) * ROW, WY)],
-                sems.at[2 + i], semr.at[2 + i], (east, r)))
+                sems, semr, (east, r)))
         return copies
 
     corners_from = [FIRST * ROW, FIRST * ROW + WY - 1, (FIRST + WX - 1) * ROW, (FIRST + WX - 1) * ROW + WY - 1]
@@ -208,32 +208,40 @@
     has_south = (r > 0).astype(jnp.float32)
     has_north = (r < PARTS - 1).astype(jnp.float32)
 
-    def send_halo(step, group, first_tile, count):
-        for n in range(count):
+    def send_halo(step, group):
+        first_tile, count = GROUPS[group]
+
+        def one(n, carry):
             t = first_tile + n
             for side, start in enumerate((0, WY - 2)):
                 for i in range(2):
-                    ysend[step, group, side, n, i] = ext[step, t, pl.ds(FIRST * ROW + start + i, WX, stride=ROW), :]
+                    ysend[step, side, t, i] = ext[step, t, pl.ds(FIRST * ROW + start + i, WX, stride=ROW), :]
             for k in range(4):
                 csend[step, group, k, pl.ds(n, 1), :] = ext[step, t, pl.ds(corners_from[k], 1), :]
-        for copy in halo_copies(step, group, first_tile, count):
+            return carry
+
+        lax.fori_loop(0, count, one, 0)
+        for copy in halo_copies(step, group):
             copy.start()
 
-    def take_halo(step, group, first_tile, count):
-        for copy in halo_copies(step, group, first_tile, count):
-            copy.wait()
-        for n in range(count):
+    def take_halo(step, group):
+        first_tile, count = GROUPS[group]
+        drain(halo_recv.at[step, group], count * (4 * WY + 2 * SMALL) + 4 * 8)
+
+        def one(n, carry):
             t = first_tile + n
             for i in range(2):
-                ext[step, t, pl.ds(FIRST * ROW - 2 + i, WX, stride=ROW), :] = yrecv[step, group, 0, n, i] * has_south
-                ext[step, t, pl.ds(FIRST * ROW + WY + i, WX, stride=ROW), :] = yrecv[step, group, 1, n, i] * has_north
+                ext[step, t, pl.ds(FIRST * ROW - 2 + i, WX, stride=ROW), :] = yrecv[step, 0, t, i] * has_south
+                ext[step, t, pl.ds(FIRST * ROW + WY + i, WX, stride=ROW), :] = yrecv[step, 1, t, i] * has_north
             for k in range(4):
                 inside = has_south if k % 2 == 0 else has_north
                 ext[step, t, pl.ds(corners_to[k], 1), :] = crecv[step, group, k, pl.ds(n, 1), :] * inside
+            return carry
+
+        lax.fori_loop(0, count, one, 0)
 
     def turn(t):
-        for copy in entry_copies(t):
-            copy.wait()
+        drain(in_recv.at[t], (PARTS - 1) * 2 * SHARE)
         for half in range(2):
             block = flat[t, half].T
             for i in range(4):
@@ -269,7 +277,7 @@
             for n in range(count):
                 t = first_tile + n
                 cx, cy = speeds(t)
-                e1[t, pl.ds(at, 16), :] = advance(cx, cy, lambda a: ext[step, t, pl.ds(a, 16), :], at, sea_here)
+                e1[pl.ds(pl.multiple_of(t * EXT + at, 8), 16), :] = advance(cx, cy, lambda a: ext[step, t, pl.ds(a, 16), :], at, sea_here)
             return c
 
         lax.fori_loop(2 * ROW // 16, 12 * ROW // 16, first, 0)
@@ -282,7 +290,7 @@
             for n in range(count):
                 t = first_tile + n
                 cx, cy = speeds(t)
-                new = advance(cx, cy, lambda a: e1[t, pl.ds(a, 16), :], at, sea_here)
+                new = advance(cx, cy, lambda a: e1[pl.ds(t * EXT + a, 16), :], at, sea_here)
                 e2[t, to, :] = new
                 square = new * new
                 squares += square
@@ -310,10 +318,10 @@
                     out[pl.ds(128 * t + SHARE * k, SHARE), tile_rows(v)] = block[i * SHARE:(i + 1) * SHARE]
 
     turn(OT)
-    send_halo(0, GROUPS - 1, OT, 1)
-
-    for copy in sea_copies:
-        copy.wait()
+    send_halo(0, 3)
+
+    drain(sea_recv.at[0], 2 * 16)
+    drain(sea_send.at[0], 2 * 16)
     sea_turned[...] = jnp.zeros_like(sea_turned)
     for h in range(2):
         lanes = slice(h * 128, (h + 1) * 128)
@@ -327,39 +335,55 @@
         left = sea_turned[pl.ds(6 + r * WY, 2), :]
         sea_ext[pl.ds((q + 1) * ROW - 2, 2), :] = jnp.broadcast_to(left[:, column:column + 1], (2, 128))
 
-    for copy in weights:
-        copy.wait()
+    pltpu.make_async_copy(dk_raw, dk_raw, weights_sem.at[0]).wait()
     for u in range(LT):
         block = dk_raw[:, u * 128:(u + 1) * 128].T
         for i in range(8):
             k, t = divmod(8 * u + i, LT)
             wd[pl.ds(128 * t + SHARE * k, SHARE), :] = block[i * SHARE:(i + 1) * SHARE]
 
-    take_halo(0, GROUPS - 1, OT, 1)
-    currents(0)
-    total[...] = jnp.zeros_like(total)
-
-    def enter_pair(n, c):
-        turn(2 * n)
-        turn(2 * n + 1)
-        send_halo(0, n, 2 * n, 2)
-        prepare(2 * n)
-        prepare(2 * n + 1)
-
-        @pl.when(n > 0)
+    def advect_pairs(step, group):
+        take_halo(step, group)
+        begin, count = GROUPS[group]
+
+        def one(n, c):
+            advect(step, 2 * n, 2)
+            return c
+
+        lax.fori_loop(begin // 2, (begin + count) // 2, one, 0)
+
+    def wake(step):
+        take_halo(step, 3)
+        currents(step)
+        total[...] = jnp.zeros_like(total)
+
+    pltpu.make_async_copy(kl_raw, kl_raw, weights_sem.at[1]).wait()
+    pltpu.make_async_copy(ks_raw, ks_raw, weights_sem.at[2]).wait()
+
+    def enter_tile(t, c):
+        turn(t)
+
+        @pl.when(t == 3)
         def _():
-            take_halo(0, n - 1, 2 * n - 2, 2)
-            advect(0, 2 * n - 2, 2)
+            send_halo(0, 0)
+
+        @pl.when(t == 7)
+        def _():
+            send_halo(0, 1)
+
+        prepare(t)
+
+        @pl.when(t == 5)
+        def _():
+            wake(0)
+            advect_pairs(0, 0)
 
         return c
 
-    lax.fori_loop(0, LT // 2, enter_pair, 0)
-    turn(LT - 1)
-    send_halo(0, GROUPS - 2, LT - 1, 1)
-    prepare(LT - 1)
-    take_halo(0, GROUPS - 3, LT - 3, 2)
-    advect(0, LT - 3, 2)
-    take_halo(0, GROUPS - 2, LT - 1, 1)
+    lax.fori_loop(0, LT, enter_tile, 0)
+    send_halo(0, 2)
+    advect_pairs(0, 1)
+    take_halo(0, 2)
     advect(0, LT - 1, 1)
 
     lane_row = lax.broadcasted_iota(jnp.int32, (WY, 128), 1)
@@ -374,7 +398,7 @@
         for half in range(2):
             got[t, r, half] = back[t, half, share_rows(r), :]
 
-    def source(step, first_tile, count, group, now):
+    def source(step, first_tile, count, last):
         lanes = pl.ds(pl.multiple_of(first_tile * 128, 128), count * 128)
         inter = jnp.dot(rounded[...], wl[:, lanes], preferred_element_type=jnp.float32)
         inter += jnp.dot(squared[...], ws[:, lanes], preferred_element_type=jnp.float32)
@@ -382,20 +406,16 @@
         for k in range(count):
             old = e2[first_tile + k]
             new = old + inter[:, k * 128:(k + 1) * 128] * old * weight[...]
-            if step < STEPS - 1:
+            if last:
+                turn_back(first_tile + k, new)
+            else:
                 for x in range(WX):
                     ext[step + 1, first_tile + k, pl.ds((FIRST + x) * ROW, WY), :] = new[x * WY:(x + 1) * WY]
-            else:
-                turn_back(first_tile + k, new)
             fresh.append(new.astype(jnp.bfloat16))
         fresh = jnp.concatenate(fresh, axis=1) if count > 1 else fresh[0]
         drift[...] += jnp.dot(fresh, wd[lanes, :], preferred_element_type=jnp.float32)
-        if step < STEPS - 1 and now is not None:
-            @pl.when(now)
-            def _():
-                send_halo(step + 1, group, first_tile, count)
-
-    def swim(step):
+
+    def swim(step, last):
         def one(x, c):
             at = own_row(x)
             old = ext[step, OT, pl.ds(at, WY), :]
@@ -405,51 +425,47 @@
             pushed = old + drift[here, :]
             other = jnp.where(even, pltpu.roll(pushed, 127, 1), pltpu.roll(pushed, 1, 1))
             new = (old + (sign * other + DT_OCEAN * lap)) * sea_ext[pl.ds(at, WY), :]
-            if step < STEPS - 1:
+            if last:
+                drift[here, :] = new
+            else:
                 ext[step + 1, OT, pl.ds(at, WY), :] = new
-            else:
-                drift[here, :] = new
             return c
         lax.fori_loop(0, WX, one, 0)
-        if step == STEPS - 1:
+        if last:
             turn_back(OT, drift[...])
 
-    for step in range(STEPS):
-        if step:
-            take_halo(step, GROUPS - 1, OT, 1)
-            currents(step)
-            total[...] = jnp.zeros_like(total)
-
-            def advect_pair(n, c):
-                take_halo(step, n, 2 * n, 2)
-                advect(step, 2 * n, 2)
-                return c
-
-            lax.fori_loop(0, LT // 2, advect_pair, 0)
-            take_halo(step, GROUPS - 2, LT - 1, 1)
-            advect(step, LT - 1, 1)
+    def react(step, last):
         weigh()
         drift[...] = jnp.zeros_like(drift)
 
         def source_pair(n, c):
-            source(step, 2 * n, 2, n, n < HOLD)
+            source(step, 2 * n, 2, last)
+            if not last:
+                @pl.when(n == 1)
+                def _():
+                    send_halo(step + 1, 0)
             return c
 
         lax.fori_loop(0, LT // 2, source_pair, 0)
-        source(step, LT - 1, 1, None, None)
-        swim(step)
-        if step < STEPS - 1:
-            send_halo(step + 1, GROUPS - 1, OT, 1)
-            for n in range(HOLD, LT // 2):
-                send_halo(step + 1, n, 2 * n, 2)
-            send_halo(step + 1, GROUPS - 2, LT - 1, 1)
-
-    def spec_store(t, h):
-        return pltpu.make_async_copy(spec_out.at[h, tile_rows(t)], eo.at[tile_rows(t), half_lanes(h)], store.at[t, h])
+        source(step, LT - 1, 1, last)
+        swim(step, last)
+
+    def whole_step(step, c):
+        react(step, False)
+        for group in (3, 1, 2):
+            send_halo(step + 1, group)
+        wake(step + 1)
+        advect_pairs(step + 1, 0)
+        advect_pairs(step + 1, 1)
+        take_halo(step + 1, 2)
+        advect(step + 1, LT - 1, 1)
+        return c
+
+    lax.fori_loop(0, STEPS - 1, whole_step, 0)
+    react(STEPS - 1, True)
 
     def leave(t, carry):
-        for copy in exit_copies(t):
-            copy.wait()
+        drain(out_recv.at[t], (PARTS - 1) * 2 * SHARE)
         for octet in range(2):
             for h in range(2):
                 for half in range(2):
@@ -457,26 +473,25 @@
                     for i in range(4):
                         spec_out[h, pl.ds(t * 128 + octet * 64 + 4 * half + i, 8, stride=8), :] = blocks[i]
         for h in range(2):
-            spec_store(t, h).start()
+            pltpu.make_async_copy(
+                spec_out.at[h, tile_rows(t)], eo.at[tile_rows(t), half_lanes(h)], store.at[0]).start()
         return carry
 
     lax.fori_loop(0, LT, leave, 0)
-    for copy in exit_copies(OT):
-        copy.wait()
+    drain(out_recv.at[OT], (PARTS - 1) * 2 * SHARE)
     for comp in range(2):
         for h in range(2):
             for half in range(2):
                 blocks = swap_blocks([got[OT, 4 * h + j, half, pl.ds(comp, 8, stride=2), :] for j in range(4)])
                 for i in range(4):
                     swim_out[h, pl.ds(64 * comp + 4 * half + i, 8, stride=8), :] = blocks[i]
-    stores = [pltpu.make_async_copy(swim_out.at[h], oo.at[:, half_lanes(h)], store.at[LT, h]) for h in range(2)]
-    for copy in stores:
-        copy.start()
-    for t in range(LT):
-        for h in range(2):
-            spec_store(t, h).wait()
-    for copy in stores:
-        copy.wait()
+    for h in range(2):
+        pltpu.make_async_copy(swim_out.at[h], oo.at[:, half_lanes(h)], store.at[0]).start()
+    drain(store.at[0], 2 * NB + 256)
+    drain(in_send.at[0], NT * (PARTS - 1) * 2 * SHARE)
+    drain(out_send.at[0], NT * (PARTS - 1) * 2 * SHARE)
+    for step in range(STEPS):
+        drain(halo_send.at[step], NT * (4 * WY + 2 * SMALL) + len(GROUPS) * 4 * 8)
 
 
 def per_device(spectrum, sea_mask, kernel_linear, kernel_square, drift_kernel, ocean):
@@ -499,7 +514,7 @@
             pltpu.VMEM((3, 8, y), f32),
             pltpu.VMEM((8 + 256 + ROW, 128), f32),
             pltpu.VMEM((EXT, 128), f32),
-            pltpu.VMEM((LT, EXT, 128), f32),
+            pltpu.VMEM((LT * EXT, 128), f32),
             pltpu.VMEM((LT, COLS, 128), f32),
             pltpu.VMEM((COLS, NB), bf16),
             pltpu.VMEM((COLS, NB), bf16),
@@ -514,25 +529,25 @@
             pltpu.VMEM((NB, NB), bf16),
             pltpu.VMEM((NB, NB), bf16),
             pltpu.VMEM((NB, 128), bf16),
-            pltpu.VMEM((STEPS, GROUPS, 2, 2, 2, WX, 128), f32),
-            pltpu.VMEM((STEPS, GROUPS, 2, 2, 2, WX, 128), f32),
-            pltpu.VMEM((STEPS, GROUPS, 4, 8, 128), f32),
-            pltpu.VMEM((STEPS, GROUPS, 4, 8, 128), f32),
+            pltpu.VMEM((STEPS, 2, NT, 2, WX, 128), f32),
+            pltpu.VMEM((STEPS, 2, NT, 2, WX, 128), f32),
+            pltpu.VMEM((STEPS, len(GROUPS), 4, 8, 128), f32),
+            pltpu.VMEM((STEPS, len(GROUPS), 4, 8, 128), f32),
             pltpu.VMEM((NT, 2, 128, 128), f32),
             pltpu.VMEM((NT, PARTS, 2, SHARE, 128), f32),
             pltpu.VMEM((2, NB, 128), f32),
             pltpu.VMEM((2, 128, 128), f32),
-            dma((NT, PARTS)),
-            dma((NT, PARTS)),
-            dma((STEPS, GROUPS, 10)),
-            dma((STEPS, GROUPS, 10)),
-            dma((2,)),
-            dma((2,)),
-            dma((NT, PARTS)),
-            dma((NT, PARTS)),
-            dma((NT, 2)),
-            dma((1 + 2 * LT,)),
-            dma((NT, 2)),
+            dma((1,)),
+            dma((NT,)),
+            dma((STEPS,)),
+            dma((STEPS, len(GROUPS))),
+            dma((1,)),
+            dma((1,)),
+            dma((1,)),
+            dma((NT,)),
+            dma((NT,)),
+            dma((3,)),
+            dma((1,)),
         ],
         compiler_params=pltpu.CompilerParams(
             collective_id=0, has_side_effects=True, vmem_limit_bytes=60 * 1024 * 1024

time: 110 us -> 95 us (0.86)
  Pallas kernels: 106 us -> 91.1 us
    pallas_call x1, Pallas kernels: 106 us -> 91.1 us  [per_device(): pl.pallas_call(kernel, out_shape=(jax.ShapeDtypeStruct((NB, y), f32), jax...]
where the time goes in v3:
time: 95 us; the launch traced here: 94.8 us
  Pallas kernels  91.1 us (96%)
  local copies, waits for them, and re-layouts  3.05 us (3%)
    pallas_call x1, Pallas kernels, per_device(): pl.pallas_call(kernel, out_shape=(jax.ShapeDtypeStruct((NB, y), f32), jax...  91.1 us
    unnamed x4, local copies, waits for them, and re-layouts  3.05 us

profile of v3, /device:TPU:1, one launch (start us, length us, event | category | flops | bytes accessed | tf_op | source)
XLA Modules:
  0.0 94.8 jit_solution(14924040054272769703)
XLA Ops:
  0.6 91.1 %coupled.1 = (f32[1152,256]{1,0:T(8,128)}, f32[128,256]{1,0:T(8,128)}) custom-call(f32[1152,256]{1,0:T(8,128)} %bitcast.9, f32[128,256]{1,0:T(8,128)} %bitcast.10, s32[8,256]{1,0:T(8,128)} %sea.1, bf16[8,9,16,1152]{3,2,1,0:T(8,128)(2,1)} %bitcast.6, bf16[8,9,16,1152]{3,2,1,0:T(8,128)(2,1)} %bitcast.7, bf16[128,1152]{1,0:T(8,128)(2,1)} %dk.1, ...), custom_call_target="tpu_custom_call" | custom-call | tf_op jit(solution)/shard_map/coupled/pallas_call | solution.py:503
  91.7 0.0 copy-start
  91.7 2.4 %copy.11 = f32[144,8,256]{2,1,0:T(8,128)} copy(f32[144,8,256]{2,1,0:T(8,128)} %bitcast.8) | data formatting | bytes 2359296
  94.1 0.0 copy-done
  94.1 0.7 copy.12
Async XLA Ops:
  91.7 2.4 %copy-start = (f32[128,256]{1,0:T(8,128)S(1)}, f32[128,256]{1,0:T(8,128)}, u32[]{:S(2)}) copy-start(f32[128,256]{1,0:T(8,128)} %get-tuple-element.5) | copy-start | bytes 393220

commit v4 on v3

--- a/solution.py
+++ b/solution.py
@@ -19,12 +19,16 @@
 LT = NB // 128
 OT = LT
 NT = LT + 1
-GROUPS = ((0, 4), (4, 4), (8, 1), (OT, 1))
+PAIRS = LT // 2
+SIDES = ((0, 4), (4, 4), (LT - 1, 1), (OT, 1))
+OCEAN = len(SIDES) - 1
 SMALL = WX * 2
 ROW = 40
 ROWS = 13
 EXT = ROW * ROWS
 FIRST = 3
+INSIDE = (FIRST + 1) * ROW
+OUTSIDE = (FIRST + WX - 2) * ROW + 24
 
 DT_SOURCE = 0.5
 DT_OCEAN = 0.2
@@ -177,39 +181,35 @@
     pltpu.make_async_copy(dk, dk_raw, weights_sem.at[0]).start()
     lax.fori_loop(0, LT, weights_load, 0)
 
-    def halo_copies(step, group):
-        first_tile, count = GROUPS[group]
+    def rows_arrived(step, pair):
+        return halo_recv.at[step, pair]
+
+    def columns_arrived(step, group):
+        return halo_recv.at[step, PAIRS + 1 + group]
+
+    def corners_arrived(step, group):
+        return halo_recv.at[step, PAIRS + 1 + len(SIDES) + group]
+
+    def send_rows(step, first_tile, count, arrived):
         field = ext.at[step]
         every = pl.ds(first_tile, count)
-        sems, semr = halo_send.at[step], halo_recv.at[step, group]
-        ys, yr = ysend.at[step], yrecv.at[step]
-        cs, cr = csend.at[step, group], crecv.at[step, group]
-        copies = [
-            remote(ys.at[0, every], yr.at[1, every], sems, semr, (g, south)),
-            remote(ys.at[1, every], yr.at[0, every], sems, semr, (g, north)),
-            remote(cs.at[0], cr.at[3], sems, semr, (west, south)),
-            remote(cs.at[1], cr.at[2], sems, semr, (west, north)),
-            remote(cs.at[2], cr.at[1], sems, semr, (east, south)),
-            remote(cs.at[3], cr.at[0], sems, semr, (east, north)),
-        ]
         for i in range(2):
-            copies.append(remote(
+            remote(
                 field.at[every, pl.ds((FIRST + i) * ROW, WY)],
                 field.at[every, pl.ds((FIRST + WX + i) * ROW, WY)],
-                sems, semr, (west, r)))
-            copies.append(remote(
+                halo_send.at[step], arrived, (west, r)).start()
+            remote(
                 field.at[every, pl.ds((FIRST + WX - 2 + i) * ROW, WY)],
                 field.at[every, pl.ds((FIRST - 2 + i) * ROW, WY)],
-                sems, semr, (east, r)))
-        return copies
+                halo_send.at[step], arrived, (east, r)).start()
 
     corners_from = [FIRST * ROW, FIRST * ROW + WY - 1, (FIRST + WX - 1) * ROW, (FIRST + WX - 1) * ROW + WY - 1]
     corners_to = [(FIRST - 1) * ROW - 1, (FIRST - 1) * ROW + WY, (FIRST + WX) * ROW - 1, (FIRST + WX) * ROW + WY]
     has_south = (r > 0).astype(jnp.float32)
     has_north = (r < PARTS - 1).astype(jnp.float32)
 
-    def send_halo(step, group):
-        first_tile, count = GROUPS[group]
+    def send_sides(step, group):
+        first_tile, count = SIDES[group]
 
         def one(n, carry):
             t = first_tile + n
@@ -221,24 +221,52 @@
             return carry
 
         lax.fori_loop(0, count, one, 0)
-        for copy in halo_copies(step, group):
-            copy.start()
-
-    def take_halo(step, group):
-        first_tile, count = GROUPS[group]
-        drain(halo_recv.at[step, group], count * (4 * WY + 2 * SMALL) + 4 * 8)
+        every = pl.ds(first_tile, count)
+        columns, corners = columns_arrived(step, group), corners_arrived(step, group)
+        ys, yr = ysend.at[step], yrecv.at[step]
+        cs, cr = csend.at[step, group], crecv.at[step, group]
+        for src, dst, arrived, device in (
+            (ys.at[0, every], yr.at[1, every], columns, (g, south)),
+            (ys.at[1, every], yr.at[0, every], columns, (g, north)),
+            (cs.at[0], cr.at[3], corners, (west, south)),
+            (cs.at[1], cr.at[2], corners, (west, north)),
+            (cs.at[2], cr.at[1], corners, (east, south)),
+            (cs.at[3], cr.at[0], corners, (east, north)),
+        ):
+            remote(src, dst, halo_send.at[step], arrived, device).start()
+
+    def take_rows(step, pair, count):
+        drain(rows_arrived(step, pair), count * 4 * WY)
+
+    def take_columns(step, group):
+        first_tile, count = SIDES[group]
+        drain(columns_arrived(step, group), count * 2 * SMALL)
 
         def one(n, carry):
             t = first_tile + n
             for i in range(2):
                 ext[step, t, pl.ds(FIRST * ROW - 2 + i, WX, stride=ROW), :] = yrecv[step, 0, t, i] * has_south
                 ext[step, t, pl.ds(FIRST * ROW + WY + i, WX, stride=ROW), :] = yrecv[step, 1, t, i] * has_north
+            return carry
+
+        lax.fori_loop(0, count, one, 0)
+
+    def take_corners(step, group):
+        first_tile, count = SIDES[group]
+        drain(corners_arrived(step, group), 4 * 8 + (4 * WY if group == OCEAN else 0))
+
+        def one(n, carry):
+            t = first_tile + n
             for k in range(4):
                 inside = has_south if k % 2 == 0 else has_north
                 ext[step, t, pl.ds(corners_to[k], 1), :] = crecv[step, group, k, pl.ds(n, 1), :] * inside
             return carry
 
         lax.fori_loop(0, count, one, 0)
+
+    def send_ocean(step):
+        send_sides(step, OCEAN)
+        send_rows(step, OT, 1, corners_arrived(step, OCEAN))
 
     def turn(t):
         drain(in_recv.at[t], (PARTS - 1) * 2 * SHARE)
@@ -247,14 +275,30 @@
             for i in range(4):
                 ext[0, t, pl.ds((FIRST + 4 * half + i) * ROW, WY), :] = block[i * WY:(i + 1) * WY]
 
-    def currents(step):
-        def one(row, c):
-            at = pl.multiple_of(row * ROW, 8)
-            top = DOPPLER * jnp.tanh(ext[step, OT, pl.ds(at, ROW), :])
-            tu[pl.ds(at, ROW), :] = jnp.broadcast_to(top[:, 0:1], (ROW, 128))
-            tv[pl.ds(at, ROW), :] = jnp.broadcast_to(top[:, 1:2], (ROW, 128))
-            return c
-        lax.fori_loop(1, ROWS, one, 0)
+    def current(step, at, size):
+        top = DOPPLER * jnp.tanh(ext[step, OT, pl.ds(at, size), :])
+        tu[pl.ds(at, size), :] = jnp.broadcast_to(top[:, 0:1], (size, 128))
+        tv[pl.ds(at, size), :] = jnp.broadcast_to(top[:, 1:2], (size, 128))
+
+    def own_currents(step):
+        def one(x, c):
+            current(step, own_row(x), WY)
+            return c
+        lax.fori_loop(0, WX, one, 0)
+
+    def column_currents(step):
+        take_columns(step, OCEAN)
+
+        def one(x, c):
+            current(step, pl.multiple_of(own_row(x) + WY, 8), ROW - WY)
+            return c
+        lax.fori_loop(0, WX - 1, one, 0)
+
+    def row_currents(step):
+        take_corners(step, OCEAN)
+        for row in (1, 2, FIRST + WX, FIRST + WX + 1):
+            current(step, row * ROW, ROW)
+        current(step, (FIRST + WX - 1) * ROW + WY, ROW - WY)
 
     u_at = lambda at: tu[pl.ds(at, 16), :]
     v_at = lambda at: tv[pl.ds(at, 16), :]
@@ -267,20 +311,28 @@
         new -= jnp.minimum(cy + v_at(here + 1), 0.0) * e_at(here + 1)
         return new * sea_here
 
-    def advect(step, first_tile, count):
-        def speeds(t):
-            return jnp.concatenate([cg[0, t]] * 2, axis=0), jnp.concatenate([cg[1, t]] * 2, axis=0)
-
+    def speeds(t):
+        return jnp.concatenate([cg[0, t]] * 2, axis=0), jnp.concatenate([cg[1, t]] * 2, axis=0)
+
+    def first_substep(step, first_tile, count, start, stop):
         def first(i, c):
             at = pl.multiple_of(i * 16, 16)
             sea_here = sea_ext[pl.ds(at, 16), :]
             for n in range(count):
                 t = first_tile + n
                 cx, cy = speeds(t)
-                e1[pl.ds(pl.multiple_of(t * EXT + at, 8), 16), :] = advance(cx, cy, lambda a: ext[step, t, pl.ds(a, 16), :], at, sea_here)
-            return c
-
-        lax.fori_loop(2 * ROW // 16, 12 * ROW // 16, first, 0)
+                e1[pl.ds(pl.multiple_of(t * EXT + at, 8), 16), :] = advance(
+                    cx, cy, lambda a: ext[step, t, pl.ds(a, 16), :], at, sea_here)
+            return c
+
+        lax.fori_loop(start // 16, stop // 16, first, 0)
+
+    def advect_inside(step, first_tile, count):
+        first_substep(step, first_tile, count, INSIDE, OUTSIDE)
+
+    def advect(step, first_tile, count):
+        first_substep(step, first_tile, count, 2 * ROW, INSIDE)
+        first_substep(step, first_tile, count, OUTSIDE, 12 * ROW)
 
         def second(i, c):
             at = pl.multiple_of(own_row(lax.div(i, 2)) + lax.rem(i, 2) * 16, 8)
@@ -318,7 +370,8 @@
                     out[pl.ds(128 * t + SHARE * k, SHARE), tile_rows(v)] = block[i * SHARE:(i + 1) * SHARE]
 
     turn(OT)
-    send_halo(0, 3)
+    send_ocean(0)
+    own_currents(0)
 
     drain(sea_recv.at[0], 2 * 16)
     drain(sea_send.at[0], 2 * 16)
@@ -342,49 +395,65 @@
             k, t = divmod(8 * u + i, LT)
             wd[pl.ds(128 * t + SHARE * k, SHARE), :] = block[i * SHARE:(i + 1) * SHARE]
 
-    def advect_pairs(step, group):
-        take_halo(step, group)
-        begin, count = GROUPS[group]
-
+    def inside_pairs(step, begin, end):
         def one(n, c):
+            advect_inside(step, 2 * n, 2)
+            return c
+        lax.fori_loop(begin, end, one, 0)
+
+    def advect_pairs(step, begin, end):
+        def one(n, c):
+            take_rows(step, n, 2)
             advect(step, 2 * n, 2)
             return c
-
-        lax.fori_loop(begin // 2, (begin + count) // 2, one, 0)
-
-    def wake(step):
-        take_halo(step, 3)
-        currents(step)
-        total[...] = jnp.zeros_like(total)
+        lax.fori_loop(begin, end, one, 0)
+
+    def advect_last(step):
+        take_rows(step, PAIRS, 1)
+        advect(step, LT - 1, 1)
 
     pltpu.make_async_copy(kl_raw, kl_raw, weights_sem.at[1]).wait()
     pltpu.make_async_copy(ks_raw, ks_raw, weights_sem.at[2]).wait()
 
     def enter_tile(t, c):
+        prepare(t)
         turn(t)
+
+        @pl.when(lax.rem(t, 2) == 1)
+        def _():
+            send_rows(0, t - 1, 2, rows_arrived(0, lax.div(t, 2)))
 
         @pl.when(t == 3)
         def _():
-            send_halo(0, 0)
+            send_sides(0, 0)
 
         @pl.when(t == 7)
         def _():
-            send_halo(0, 1)
-
-        prepare(t)
+            send_sides(0, 1)
 
         @pl.when(t == 5)
         def _():
-            wake(0)
-            advect_pairs(0, 0)
+            column_currents(0)
+            take_columns(0, 0)
+            inside_pairs(0, 0, 2)
+            row_currents(0)
+            take_corners(0, 0)
+            advect_pairs(0, 0, 2)
 
         return c
 
+    total[...] = jnp.zeros_like(total)
     lax.fori_loop(0, LT, enter_tile, 0)
-    send_halo(0, 2)
-    advect_pairs(0, 1)
-    take_halo(0, 2)
-    advect(0, LT - 1, 1)
+    send_sides(0, 2)
+    send_rows(0, LT - 1, 1, rows_arrived(0, PAIRS))
+    take_columns(0, 1)
+    inside_pairs(0, 2, PAIRS)
+    take_corners(0, 1)
+    advect_pairs(0, 2, PAIRS)
+    take_columns(0, 2)
+    advect_inside(0, LT - 1, 1)
+    take_corners(0, 2)
+    advect_last(0)
 
     lane_row = lax.broadcasted_iota(jnp.int32, (WY, 128), 1)
     even = lax.rem(lane_row, 2) == 0
@@ -441,9 +510,13 @@
         def source_pair(n, c):
             source(step, 2 * n, 2, last)
             if not last:
+                @pl.when(n < 2)
+                def _():
+                    send_rows(step + 1, 2 * n, 2, rows_arrived(step + 1, n))
+
                 @pl.when(n == 1)
                 def _():
-                    send_halo(step + 1, 0)
+                    send_sides(step + 1, 0)
             return c
 
         lax.fori_loop(0, LT // 2, source_pair, 0)
@@ -452,13 +525,25 @@
 
     def whole_step(step, c):
         react(step, False)
-        for group in (3, 1, 2):
-            send_halo(step + 1, group)
-        wake(step + 1)
-        advect_pairs(step + 1, 0)
-        advect_pairs(step + 1, 1)
-        take_halo(step + 1, 2)
-        advect(step + 1, LT - 1, 1)
+        send_ocean(step + 1)
+        send_sides(step + 1, 1)
+        send_sides(step + 1, 2)
+        for n in range(2, PAIRS):
+            send_rows(step + 1, 2 * n, 2, rows_arrived(step + 1, n))
+        send_rows(step + 1, LT - 1, 1, rows_arrived(step + 1, PAIRS))
+        later = step + 1
+        own_currents(later)
+        column_currents(later)
+        total[...] = jnp.zeros_like(total)
+        for group in range(OCEAN):
+            take_columns(later, group)
+        inside_pairs(later, 0, PAIRS)
+        advect_inside(later, LT - 1, 1)
+        row_currents(later)
+        for group in range(OCEAN):
+            take_corners(later, group)
+        advect_pairs(later, 0, PAIRS)
+        advect_last(later)
         return c
 
     lax.fori_loop(0, STEPS - 1, whole_step, 0)
@@ -491,7 +576,7 @@
     drain(in_send.at[0], NT * (PARTS - 1) * 2 * SHARE)
     drain(out_send.at[0], NT * (PARTS - 1) * 2 * SHARE)
     for step in range(STEPS):
-        drain(halo_send.at[step], NT * (4 * WY + 2 * SMALL) + len(GROUPS) * 4 * 8)
+        drain(halo_send.at[step], NT * (4 * WY + 2 * SMALL) + len(SIDES) * 4 * 8)
 
 
 def per_device(spectrum, sea_mask, kernel_linear, kernel_square, drift_kernel, ocean):
@@ -531,8 +616,8 @@
             pltpu.VMEM((NB, 128), bf16),
             pltpu.VMEM((STEPS, 2, NT, 2, WX, 128), f32),
             pltpu.VMEM((STEPS, 2, NT, 2, WX, 128), f32),
-            pltpu.VMEM((STEPS, len(GROUPS), 4, 8, 128), f32),
-            pltpu.VMEM((STEPS, len(GROUPS), 4, 8, 128), f32),
+            pltpu.VMEM((STEPS, len(SIDES), 4, 8, 128), f32),
+            pltpu.VMEM((STEPS, len(SIDES), 4, 8, 128), f32),
             pltpu.VMEM((NT, 2, 128, 128), f32),
             pltpu.VMEM((NT, PARTS, 2, SHARE, 128), f32),
             pltpu.VMEM((2, NB, 128), f32),
@@ -540,7 +625,7 @@
             dma((1,)),
             dma((NT,)),
             dma((STEPS,)),
-            dma((STEPS, len(GROUPS))),
+            dma((STEPS, PAIRS + 1 + 2 * len(SIDES))),
             dma((1,)),
             dma((1,)),
             dma((1,)),

time: 95 us -> 89.8 us (0.945)
  Pallas kernels: 91.1 us -> 85.9 us
    pallas_call x1, Pallas kernels: 91.1 us -> 85.9 us  [per_device(): pl.pallas_call(kernel, out_shape=(jax.ShapeDtypeStruct((NB, y), f32), jax...]
where the time goes in v4:
time: 89.8 us; the launch traced here: 89.6 us
  Pallas kernels  85.9 us (96%)
  local copies, waits for them, and re-layouts  3.05 us (3%)
    pallas_call x1, Pallas kernels, per_device(): pl.pallas_call(kernel, out_shape=(jax.ShapeDtypeStruct((NB, y), f32), jax...  85.9 us
    unnamed x4, local copies, waits for them, and re-layouts  3.05 us

profile of v4, /device:TPU:1, one launch (start us, length us, event | category | flops | bytes accessed | tf_op | source)
XLA Modules:
  0.0 89.6 jit_solution(5663526403368263424)
XLA Ops:
  0.6 85.9 %coupled.1 = (f32[1152,256]{1,0:T(8,128)}, f32[128,256]{1,0:T(8,128)}) custom-call(f32[1152,256]{1,0:T(8,128)} %bitcast.9, f32[128,256]{1,0:T(8,128)} %bitcast.10, s32[8,256]{1,0:T(8,128)} %sea.1, bf16[8,9,16,1152]{3,2,1,0:T(8,128)(2,1)} %bitcast.6, bf16[8,9,16,1152]{3,2,1,0:T(8,128)(2,1)} %bitcast.7, bf16[128,1152]{1,0:T(8,128)(2,1)} %dk.1, ...), custom_call_target="tpu_custom_call" | custom-call | tf_op jit(solution)/shard_map/coupled/pallas_call | solution.py:588
  86.5 0.0 copy-start
  86.5 2.4 %copy.11 = f32[144,8,256]{2,1,0:T(8,128)} copy(f32[144,8,256]{2,1,0:T(8,128)} %bitcast.8) | data formatting | bytes 2359296
  88.9 0.0 copy-done
  88.9 0.7 copy.12
Async XLA Ops:
  86.5 2.4 %copy-start = (f32[128,256]{1,0:T(8,128)S(1)}, f32[128,256]{1,0:T(8,128)}, u32[]{:S(2)}) copy-start(f32[128,256]{1,0:T(8,128)} %get-tuple-element.5) | copy-start | bytes 393220

commit v5 on v4

--- a/solution.py
+++ b/solution.py
@@ -431,21 +431,18 @@
         def _():
             send_sides(0, 1)
 
-        @pl.when(t == 5)
-        def _():
-            column_currents(0)
-            take_columns(0, 0)
-            inside_pairs(0, 0, 2)
-            row_currents(0)
-            take_corners(0, 0)
-            advect_pairs(0, 0, 2)
-
         return c
 
     total[...] = jnp.zeros_like(total)
     lax.fori_loop(0, LT, enter_tile, 0)
     send_sides(0, 2)
     send_rows(0, LT - 1, 1, rows_arrived(0, PAIRS))
+    column_currents(0)
+    take_columns(0, 0)
+    inside_pairs(0, 0, 2)
+    row_currents(0)
+    take_corners(0, 0)
+    advect_pairs(0, 0, 2)
     take_columns(0, 1)
     inside_pairs(0, 2, PAIRS)
     take_corners(0, 1)

time: 89.8 us -> 85.8 us (0.955)
  Pallas kernels: 85.9 us -> 81.9 us
    pallas_call x1, Pallas kernels: 85.9 us -> 81.9 us  [per_device(): pl.pallas_call(kernel, out_shape=(jax.ShapeDtypeStruct((NB, y), f32), jax...]
where the time goes in v5:
time: 85.8 us; the launch traced here: 85.6 us
  Pallas kernels  81.9 us (95%)
  local copies, waits for them, and re-layouts  3.05 us (4%)
    pallas_call x1, Pallas kernels, per_device(): pl.pallas_call(kernel, out_shape=(jax.ShapeDtypeStruct((NB, y), f32), jax...  81.9 us
    unnamed x4, local copies, waits for them, and re-layouts  3.05 us

profile of v5, /device:TPU:1, one launch (start us, length us, event | category | flops | bytes accessed | tf_op | source)
XLA Modules:
  0.0 85.6 jit_solution(2240552786710306667)
XLA Ops:
  0.6 81.9 %coupled.1 = (f32[1152,256]{1,0:T(8,128)}, f32[128,256]{1,0:T(8,128)}) custom-call(f32[1152,256]{1,0:T(8,128)} %bitcast.9, f32[128,256]{1,0:T(8,128)} %bitcast.10, s32[8,256]{1,0:T(8,128)} %sea.1, bf16[8,9,16,1152]{3,2,1,0:T(8,128)(2,1)} %bitcast.6, bf16[8,9,16,1152]{3,2,1,0:T(8,128)(2,1)} %bitcast.7, bf16[128,1152]{1,0:T(8,128)(2,1)} %dk.1, ...), custom_call_target="tpu_custom_call" | custom-call | tf_op jit(solution)/shard_map/coupled/pallas_call | solution.py:585
  82.5 0.0 copy-start
  82.5 2.4 %copy.11 = f32[144,8,256]{2,1,0:T(8,128)} copy(f32[144,8,256]{2,1,0:T(8,128)} %bitcast.8) | data formatting | bytes 2359296
  84.9 0.0 copy-done
  84.9 0.7 copy.12
Async XLA Ops:
  82.5 2.4 %copy-start = (f32[128,256]{1,0:T(8,128)S(1)}, f32[128,256]{1,0:T(8,128)}, u32[]{:S(2)}) copy-start(f32[128,256]{1,0:T(8,128)} %get-tuple-element.5) | copy-start | bytes 393220

commit v6 on v5

--- a/solution.py
+++ b/solution.py
@@ -325,7 +325,11 @@
                     cx, cy, lambda a: ext[step, t, pl.ds(a, 16), :], at, sea_here)
             return c
 
-        lax.fori_loop(start // 16, stop // 16, first, 0)
+        begin, times = start // 16, (stop - start) // 16
+        if times % 2:
+            lax.fori_loop(begin, begin + times, first, 0)
+        else:
+            lax.fori_loop(0, times // 2, lambda i, c: first(begin + 2 * i + 1, first(begin + 2 * i, c)), 0)
 
     def advect_inside(step, first_tile, count):
         first_substep(step, first_tile, count, INSIDE, OUTSIDE)
@@ -351,7 +355,12 @@
             total[to, :] = squares
             return c
 
-        lax.fori_loop(0, COLS // 16, second, 0)
+        def four(i, c):
+            for j in range(4):
+                c = second(4 * i + j, c)
+            return c
+
+        lax.fori_loop(0, COLS // 64, four, 0)
 
     def weigh():
         def one(x, c):

time: 85.8 us -> 84.4 us (0.984)
  Pallas kernels: 81.9 us -> 80.5 us
    pallas_call x1, Pallas kernels: 81.9 us -> 80.5 us  [per_device(): pl.pallas_call(kernel, out_shape=(jax.ShapeDtypeStruct((NB, y), f32), jax...]
where the time goes in v6:
time: 84.4 us; the launch traced here: 84.2 us
  Pallas kernels  80.5 us (95%)
  local copies, waits for them, and re-layouts  3.05 us (4%)
    pallas_call x1, Pallas kernels, per_device(): pl.pallas_call(kernel, out_shape=(jax.ShapeDtypeStruct((NB, y), f32), jax...  80.5 us
    unnamed x4, local copies, waits for them, and re-layouts  3.05 us

profile of v6, /device:TPU:1, one launch (start us, length us, event | category | flops | bytes accessed | tf_op | source)
XLA Modules:
  0.0 84.2 jit_solution(1928492807534008422)
XLA Ops:
  0.6 80.5 %coupled.1 = (f32[1152,256]{1,0:T(8,128)}, f32[128,256]{1,0:T(8,128)}) custom-call(f32[1152,256]{1,0:T(8,128)} %bitcast.9, f32[128,256]{1,0:T(8,128)} %bitcast.10, s32[8,256]{1,0:T(8,128)} %sea.1, bf16[8,9,16,1152]{3,2,1,0:T(8,128)(2,1)} %bitcast.6, bf16[8,9,16,1152]{3,2,1,0:T(8,128)(2,1)} %bitcast.7, bf16[128,1152]{1,0:T(8,128)(2,1)} %dk.1, ...), custom_call_target="tpu_custom_call" | custom-call | tf_op jit(solution)/shard_map/coupled/pallas_call | solution.py:594
  81.1 0.0 copy-start
  81.1 2.4 %copy.11 = f32[144,8,256]{2,1,0:T(8,128)} copy(f32[144,8,256]{2,1,0:T(8,128)} %bitcast.8) | data formatting | bytes 2359296
  83.5 0.0 copy-done
  83.5 0.7 copy.12
Async XLA Ops:
  81.1 2.4 %copy-start = (f32[128,256]{1,0:T(8,128)S(1)}, f32[128,256]{1,0:T(8,128)}, u32[]{:S(2)}) copy-start(f32[128,256]{1,0:T(8,128)} %get-tuple-element.5) | copy-start | bytes 393220

commit v7 on v6

--- a/solution.py
+++ b/solution.py
@@ -327,7 +327,8 @@
 
         begin, times = start // 16, (stop - start) // 16
         if times % 2:
-            lax.fori_loop(begin, begin + times, first, 0)
+            for i in range(begin, begin + times):
+                first(i, 0)
         else:
             lax.fori_loop(0, times // 2, lambda i, c: first(begin + 2 * i + 1, first(begin + 2 * i, c)), 0)
 

time: 84.4 us -> 84 us (level)
  no operation moved by 1% of the time
where the time goes in v7:
time: 84 us; the launch traced here: 83.8 us
  Pallas kernels  80.1 us (95%)
  local copies, waits for them, and re-layouts  3.05 us (4%)
    pallas_call x1, Pallas kernels, per_device(): pl.pallas_call(kernel, out_shape=(jax.ShapeDtypeStruct((NB, y), f32), jax...  80.1 us
    unnamed x4, local copies, waits for them, and re-layouts  3.05 us

profile of v7, /device:TPU:1, one launch (start us, length us, event | category | flops | bytes accessed | tf_op | source)
XLA Modules:
  0.0 83.8 jit_solution(18232605849037817522)
XLA Ops:
  0.6 80.1 %coupled.1 = (f32[1152,256]{1,0:T(8,128)}, f32[128,256]{1,0:T(8,128)}) custom-call(f32[1152,256]{1,0:T(8,128)} %bitcast.9, f32[128,256]{1,0:T(8,128)} %bitcast.10, s32[8,256]{1,0:T(8,128)} %sea.1, bf16[8,9,16,1152]{3,2,1,0:T(8,128)(2,1)} %bitcast.6, bf16[8,9,16,1152]{3,2,1,0:T(8,128)(2,1)} %bitcast.7, bf16[128,1152]{1,0:T(8,128)(2,1)} %dk.1, ...), custom_call_target="tpu_custom_call" | custom-call | tf_op jit(solution)/shard_map/coupled/pallas_call | solution.py:595
  80.8 0.0 copy-start
  80.8 2.4 %copy.11 = f32[144,8,256]{2,1,0:T(8,128)} copy(f32[144,8,256]{2,1,0:T(8,128)} %bitcast.8) | data formatting | bytes 2359296
  83.2 0.0 copy-done
  83.2 0.7 copy.12
Async XLA Ops:
  80.8 2.4 %copy-start = (f32[128,256]{1,0:T(8,128)S(1)}, f32[128,256]{1,0:T(8,128)}, u32[]{:S(2)}) copy-start(f32[128,256]{1,0:T(8,128)} %get-tuple-element.5) | copy-start | bytes 393220
